TPU v7x, 32 devices: a whole 2x2x4 slice. The times are simulated.
32 devices in a mesh: samp: 8 (over y, x, core), head: 4 (over z).
Axes of the slice: x: 2, y: 2, z: 4, core: 2. Of those that a mesh axis runs over, the one named last changes fastest.
Arguments:
- act: bfloat16 [16, 544, 768], P('samp', 'head'), may hold values from -6 to 6
- cond: bfloat16 [16, 544, 384], P('samp', 'head'), may hold values from -6 to 6
- pair: bfloat16 [3, 544, 544, 128], P(None, 'head', 'samp'), may hold values from -6 to 6
- struct_of: int32 [16], P('samp'), may hold values from 0 to 2
- struct_len: int32 [3], replicated, may hold values from 272 to 544, as said below
- gain_first: bfloat16 [384], P('samp'), may hold values from 0.25 to 1.75
- scale_first: bfloat16 [384, 768], P('samp'), may hold values from -0.3125 to 0.3125
- scale_bias_first: bfloat16 [768], P('samp'), may hold values from -4 to 4
- shift_first: bfloat16 [384, 768], P('samp'), may hold values from -0.3125 to 0.3125
- query_weight: bfloat16 [768, 768], P('samp'), may hold values from -0.21875 to 0.21875
- query_bias: bfloat16 [768], P('samp'), may hold values from -3 to 3
- key_weight: bfloat16 [768, 768], P('samp'), may hold values from -0.21875 to 0.21875
- value_weight: bfloat16 [768, 768], P('samp'), may hold values from -0.21875 to 0.21875
- gate_weight: bfloat16 [768, 768], P('samp'), may hold values from -0.21875 to 0.21875
- output_weight: bfloat16 [768, 768], P('samp'), may hold values from -3.5 to 3.5
- pair_weight: bfloat16 [128, 16], P('samp'), may hold values from -0.5 to 0.5
- zero_first: bfloat16 [384, 768], P('samp'), may hold values from -0.3125 to 0.3125
- zero_bias_first: bfloat16 [768], P('samp'), may hold values from -2 to 1
- gain_second: bfloat16 [384], P('samp'), may hold values from 0.25 to 1.75
- scale_second: bfloat16 [384, 768], P('samp'), may hold values from -0.3125 to 0.3125
- scale_bias_second: bfloat16 [768], P('samp'), may hold values from -4 to 4
- shift_second: bfloat16 [384, 768], P('samp'), may hold values from -0.3125 to 0.3125
- swish_weight: bfloat16 [768, 1536], P('samp'), may hold values from -0.21875 to 0.21875
- linear_weight: bfloat16 [768, 1536], P('samp'), may hold values from -0.21875 to 0.21875
- down_weight: bfloat16 [1536, 768], P('samp'), may hold values from -0.3125 to 0.3125
- zero_second: bfloat16 [384, 768], P('samp'), may hold values from -0.3125 to 0.3125
- zero_bias_second: bfloat16 [768], P('samp'), may hold values from -2 to 1
- cotangent: bfloat16 [16, 544, 768], P('samp', 'head'), may hold values from -6 to 6
Outputs:
- layer_out: bfloat16 [16, 544, 768], P('samp', 'head')
- input_grad: float32 [16, 544, 768], P('samp', 'head')
- cond_grad: float32 [16, 544, 384], P('samp', 'head')
- pair_grad: float32 [3, 544, 544, 128], P(None, 'head', 'samp')
- gain_first_grad: float32 [384], P('samp')
- scale_first_grad: float32 [384, 768], P('samp')
- scale_bias_first_grad: float32 [768], P('samp')
- shift_first_grad: float32 [384, 768], P('samp')
- query_weight_grad: float32 [768, 768], P('samp')
- query_bias_grad: float32 [768], P('samp')
- key_weight_grad: float32 [768, 768], P('samp')
- value_weight_grad: float32 [768, 768], P('samp')
- gate_weight_grad: float32 [768, 768], P('samp')
- output_weight_grad: float32 [768, 768], P('samp')
- pair_weight_grad: float32 [128, 16], P('samp')
- zero_first_grad: float32 [384, 768], P('samp')
- zero_bias_first_grad: float32 [768], P('samp')
- gain_second_grad: float32 [384], P('samp')
- scale_second_grad: float32 [384, 768], P('samp')
- scale_bias_second_grad: float32 [768], P('samp')
- shift_second_grad: float32 [384, 768], P('samp')
- swish_weight_grad: float32 [768, 1536], P('samp')
- linear_weight_grad: float32 [768, 1536], P('samp')
- down_weight_grad: float32 [1536, 768], P('samp')
- zero_second_grad: float32 [384, 768], P('samp')
- zero_bias_second_grad: float32 [768], P('samp')
Inputs may be any that keep to these rules, and one draw needn't show every extreme that they name: struct_len gives each structure's token count; one structure has exactly 544 tokens.
All inputs are finite; a program needn't handle non-finite values.
Results may differ from a plain program's by a relative error of at most 0.02.
Values may be sent and summed in bfloat16 or wider, within the bound.
A program may use at most 256 MiB of HBM per device.

v0:
```python
import functools

import jax
import jax.numpy as jnp
from jax import lax
from jax.experimental import pallas as pl
from jax.experimental.pallas import tpu as pltpu
from jax.sharding import PartitionSpec as P

HEAD_DIM = 48
LANES = 128
EPSILON = 1e-05
NEG_BIG = -1000000000.0
F32 = jnp.float32
BF16 = jnp.bfloat16


def norm_rows(values):
    centered = values - jnp.mean(values, axis=-1, keepdims=True)
    variance = jnp.mean(centered * centered, axis=-1, keepdims=True)
    inverse = lax.rsqrt(variance + EPSILON)
    return (centered * inverse, inverse)


def norm_back(normed, inverse, upstream):
    mean_grad = jnp.mean(upstream, axis=-1, keepdims=True)
    mean_cross = jnp.mean(upstream * normed, axis=-1, keepdims=True)
    return inverse * (upstream - mean_grad - normed * mean_cross)


def product(left_side, right_side):
    return lax.dot_general(
        left_side, right_side, (((1,), (0,)), ((), ())), preferred_element_type=F32
    )


def back_product(upstream, right_side):
    return lax.dot_general(
        upstream, right_side, (((1,), (1,)), ((), ())), preferred_element_type=F32
    )


def outer_sum(left_side, upstream):
    return lax.dot_general(
        left_side, upstream, (((0,), (0,)), ((), ())), preferred_element_type=F32
    )


def column_sum(upstream):
    return jnp.sum(upstream.astype(F32), axis=0)


def sigmoid_slope(gate_sig):
    return gate_sig * (1.0 - gate_sig)


def head_windows(width):
    group = LANES * HEAD_DIM // 16
    group = min(group, width)
    windows = []
    for head in range(group // HEAD_DIM):
        first = head * HEAD_DIM
        last = first + HEAD_DIM - 1
        start = first // LANES * LANES
        stop = (last // LANES + 1) * LANES
        windows.append((start, stop - start, first - start))
    return (group, windows)


def head_mask(width, offset):
    lane = lax.broadcasted_iota(jnp.int32, (1, width), 1)
    return (lane >= offset) & (lane < offset + HEAD_DIM)


def dot_nt(left, right):
    return lax.dot_general(left, right, (((1,), (1,)), ((), ())), preferred_element_type=F32)


def dot_nn(left, right):
    return lax.dot_general(left, right, (((1,), (0,)), ((), ())), preferred_element_type=F32)


def dot_tn(left, right):
    return lax.dot_general(left, right, (((0,), (0,)), ((), ())), preferred_element_type=F32)


def attend_kernel(struct_ref, len_ref, q_ref, k_ref, v_ref, bias_ref, out_ref, prob_ref, acc_ref):
    sample = pl.program_id(0)
    group_at = pl.program_id(1)
    length = len_ref[struct_ref[sample]]
    keys = k_ref.shape[1]
    group, windows = head_windows(q_ref.shape[2])
    valid = lax.broadcasted_iota(jnp.int32, (1, keys), 1) < length
    acc_ref[...] = jnp.zeros_like(acc_ref)
    for at, (start, width, offset) in enumerate(windows):
        lanes = slice(start, start + width)
        mask = head_mask(width, offset)
        query = q_ref[0, :, lanes]
        query = jnp.where(mask, query, jnp.zeros_like(query))
        scores = dot_nt(query, k_ref[0, :, lanes]) * HEAD_DIM ** (-0.5) + bias_ref[
            0, at
        ].astype(F32)
        scores = jnp.where(valid, scores, NEG_BIG)
        weights = jnp.exp(scores - jnp.max(scores, axis=1, keepdims=True))
        weights = weights * (1.0 / jnp.sum(weights, axis=1, keepdims=True))
        weights = weights.astype(BF16)
        prob_ref[0, at] = weights
        mixed = dot_nn(weights, v_ref[0, :, lanes])
        acc_ref[:, lanes] += jnp.where(mask, mixed, 0.0)
    out_ref[0] = acc_ref[...].astype(BF16)


def attend(struct_of, struct_len, query, key, value, bias):
    samples, rows, width = query.shape
    keys = key.shape[1]
    heads = bias.shape[1]
    group, windows = head_windows(width)
    each = len(windows)
    return pl.pallas_call(
        attend_kernel,
        out_shape=(
            jax.ShapeDtypeStruct((samples, rows, width), BF16),
            jax.ShapeDtypeStruct((samples, heads, rows, keys), BF16),
        ),
        grid_spec=pltpu.PrefetchScalarGridSpec(
            num_scalar_prefetch=2,
            grid=(samples, heads // each),
            in_specs=[
                pl.BlockSpec((1, rows, group), lambda b, g, s, n: (b, 0, g)),
                pl.BlockSpec((1, keys, group), lambda b, g, s, n: (b, 0, g)),
                pl.BlockSpec((1, keys, group), lambda b, g, s, n: (b, 0, g)),
                pl.BlockSpec((1, each, rows, keys), lambda b, g, s, n: (s[b], g, 0, 0)),
            ],
            out_specs=[
                pl.BlockSpec((1, rows, group), lambda b, g, s, n: (b, 0, g)),
                pl.BlockSpec((1, each, rows, keys), lambda b, g, s, n: (b, g, 0, 0)),
            ],
            scratch_shapes=[pltpu.VMEM((rows, group), F32)],
        ),
        compiler_params=pltpu.CompilerParams(vmem_limit_bytes=48 << 20),
        name="attend",
    )(struct_of, struct_len, query, key, value, bias)


def attend_back_kernel(
    struct_ref, q_ref, k_ref, v_ref, do_ref, prob_ref, dq_ref, dk_ref, dv_ref, bias_ref,
    dq_acc, dk_acc, dv_acc, bias_acc,
):
    samples = q_ref.shape[0]
    structs = bias_ref.shape[0]
    group, windows = head_windows(q_ref.shape[2])
    scale = HEAD_DIM ** (-0.5)
    for sample in range(samples):
        struct = struct_ref[sample]
        dq_acc[...] = jnp.zeros_like(dq_acc)
        dk_acc[...] = jnp.zeros_like(dk_acc)
        dv_acc[...] = jnp.zeros_like(dv_acc)
        for at, (start, width, offset) in enumerate(windows):
            lanes = slice(start, start + width)
            mask = head_mask(width, offset)
            upstream = do_ref[sample, :, lanes]
            upstream = jnp.where(mask, upstream, jnp.zeros_like(upstream))
            query = q_ref[sample, :, lanes]
            query = jnp.where(mask, query, jnp.zeros_like(query))
            low = prob_ref[sample, at]
            weights = low.astype(F32)
            d_weights = dot_nt(upstream, v_ref[sample, :, lanes])
            dv_acc[:, lanes] += dot_tn(low, upstream)
            cross = weights * d_weights
            delta = jnp.sum(cross, axis=1, keepdims=True)
            d_scores = (cross - weights * delta).astype(BF16)
            dq_acc[:, lanes] += jnp.where(mask, dot_nn(d_scores, k_ref[sample, :, lanes]), 0.0)
            dk_acc[:, lanes] += dot_tn(d_scores, query)
            for slab in range(structs):
                part = jnp.where(struct == slab, 1.0, 0.0) * d_scores.astype(F32)
                if sample == 0:
                    bias_acc[slab, at] = part
                elif sample < samples - 1:
                    bias_acc[slab, at] += part
                else:
                    bias_ref[slab, at] = (bias_acc[slab, at] + part).astype(BF16)
        dq_ref[sample] = (dq_acc[...] * scale).astype(BF16)
        dk_ref[sample] = (dk_acc[...] * scale).astype(BF16)
        dv_ref[sample] = dv_acc[...].astype(BF16)


def attend_back(struct_of, structs, query, key, value, upstream, prob):
    samples, rows, width = query.shape
    keys = key.shape[1]
    heads = prob.shape[1]
    group, windows = head_windows(width)
    each = len(windows)
    return pl.pallas_call(
        attend_back_kernel,
        out_shape=(
            jax.ShapeDtypeStruct((samples, rows, width), BF16),
            jax.ShapeDtypeStruct((samples, keys, width), BF16),
            jax.ShapeDtypeStruct((samples, keys, width), BF16),
            jax.ShapeDtypeStruct((structs, heads, rows, keys), BF16),
        ),
        grid_spec=pltpu.PrefetchScalarGridSpec(
            num_scalar_prefetch=1,
            grid=(heads // each,),
            in_specs=[
                pl.BlockSpec((samples, rows, group), lambda g, s: (0, 0, g)),
                pl.BlockSpec((samples, keys, group), lambda g, s: (0, 0, g)),
                pl.BlockSpec((samples, keys, group), lambda g, s: (0, 0, g)),
                pl.BlockSpec((samples, rows, group), lambda g, s: (0, 0, g)),
                pl.BlockSpec((samples, each, rows, keys), lambda g, s: (0, g, 0, 0)),
            ],
            out_specs=[
                pl.BlockSpec((samples, rows, group), lambda g, s: (0, 0, g)),
                pl.BlockSpec((samples, keys, group), lambda g, s: (0, 0, g)),
                pl.BlockSpec((samples, keys, group), lambda g, s: (0, 0, g)),
                pl.BlockSpec((structs, each, rows, keys), lambda g, s: (0, g, 0, 0)),
            ],
            scratch_shapes=[
                pltpu.VMEM((rows, group), F32),
                pltpu.VMEM((keys, group), F32),
                pltpu.VMEM((keys, group), F32),
                pltpu.VMEM((structs, each, rows, keys), F32),
            ],
        ),
        compiler_params=pltpu.CompilerParams(vmem_limit_bytes=60 << 20),
        name="attend_back",
    )(struct_of, query, key, value, upstream, prob)


def pack_rows(pieces, columns):
    return jnp.concatenate([piece.reshape(-1, columns) for piece in pieces], axis=0)


def pack_small(pieces, columns):
    flat = jnp.concatenate([piece.reshape(-1) for piece in pieces])
    rows = -(-flat.shape[0] // columns)
    rows = -(-rows // 8) * 8
    return jnp.pad(flat, (0, rows * columns - flat.shape[0])).reshape(rows, columns)


def unpack_rows(gathered, shapes):
    whole, at = [], 0
    count, _, columns = gathered.shape
    for rows, cols in shapes:
        held = rows * cols // columns
        whole.append(gathered[:, at : at + held].reshape(count * rows, cols))
        at += held
    return whole


def unpack_small(gathered, shapes):
    whole, at = [], 0
    count = gathered.shape[0]
    flat = gathered.reshape(count, -1)
    for shape in shapes:
        size = 1
        for extent in shape:
            size *= extent
        whole.append(flat[:, at : at + size].reshape((count * shape[0],) + shape[1:]))
        at += size
    return whole


def per_device(
    act, cond, pair, struct_of, struct_len,
    gain_first, scale_first, scale_bias_first, shift_first,
    query_weight, query_bias, key_weight, value_weight, gate_weight, output_weight,
    pair_weight, zero_first, zero_bias_first,
    gain_second, scale_second, scale_bias_second, shift_second,
    swish_weight, linear_weight, down_weight, zero_second, zero_bias_second,
    cotangent,
):
    samples, rows, width = act.shape
    cond_width = cond.shape[2]
    total = samples * rows
    structs = pair.shape[0]
    small = (
        gain_first, scale_bias_first, query_bias, zero_bias_first, gain_second,
        scale_bias_second, zero_bias_second, pair_weight,
    )
    early = (scale_first, shift_first, query_weight, key_weight, value_weight, gate_weight)
    late = (
        output_weight, zero_first, scale_second, shift_second, swish_weight, linear_weight,
        down_weight, zero_second,
    )
    small_all = lax.all_gather(pack_small(small, width), "samp", axis=0)
    early_all = lax.all_gather(pack_rows(early, width), "samp", axis=0)
    late_all = lax.all_gather(pack_rows(late, width), "samp", axis=0)
    (gain_one, bias_one, bias_query, bias_zero_one, gain_two, bias_two, bias_zero_two, pair_proj_w) = (
        unpack_small(small_all, [piece.shape for piece in small])
    )
    (w_scale, w_shift, w_query, w_key, w_value, w_gate) = unpack_rows(
        early_all, [piece.shape for piece in early]
    )
    (w_out, w_zero, w_scale_two, w_shift_two, w_swish, w_linear, w_down, w_zero_two) = unpack_rows(
        late_all, [piece.shape for piece in late]
    )

    pair_normed, pair_inverse = norm_rows(pair.astype(F32))
    pair_low = pair_normed.astype(BF16)
    pair_proj = jnp.einsum("sijc,ch->shij", pair_low, pair_proj_w, preferred_element_type=F32)
    bias_all = lax.all_gather(pair_proj.astype(BF16), "samp", axis=3, tiled=True)

    act_rows = act.reshape(total, width).astype(F32)
    cond_low = cond.reshape(total, cond_width)
    act_normed, act_inverse = norm_rows(act_rows)
    cond_normed, cond_inverse = norm_rows(cond_low.astype(F32))
    cond_first = (cond_normed * gain_one.astype(F32)).astype(BF16)
    sig_first = jax.nn.sigmoid(product(cond_first, w_scale) + bias_one.astype(F32))
    adapted = (sig_first * act_normed + product(cond_first, w_shift)).astype(BF16)
    key_rows = product(adapted, w_key).astype(BF16)
    value_rows = product(adapted, w_value).astype(BF16)
    query_rows = (product(adapted, w_query) + bias_query.astype(F32)).astype(BF16)
    gate_sig = jax.nn.sigmoid(product(adapted, w_gate))
    key_value = jnp.stack((key_rows, value_rows)).reshape(2, samples, rows, width)
    key_value = lax.all_gather(key_value, "head", axis=2, tiled=True)
    query_split = query_rows.reshape(samples, rows, width)
    attended, prob = attend(
        struct_of, struct_len, query_split, key_value[0], key_value[1], bias_all
    )
    attn_float = attended.reshape(total, width).astype(F32)

    gated_rows = (gate_sig * attn_float).astype(BF16)
    branch = product(gated_rows, w_out)
    zero_sig_first = jax.nn.sigmoid(product(cond_low, w_zero) + bias_zero_one.astype(F32))
    middle = act_rows + zero_sig_first * branch
    mid_normed, mid_inverse = norm_rows(middle)
    cond_second = (cond_normed * gain_two.astype(F32)).astype(BF16)
    sig_second = jax.nn.sigmoid(product(cond_second, w_scale_two) + bias_two.astype(F32))
    adapted_two = (sig_second * mid_normed + product(cond_second, w_shift_two)).astype(BF16)
    swish_pre = product(adapted_two, w_swish)
    linear_pre = product(adapted_two, w_linear)
    swish_sig = jax.nn.sigmoid(swish_pre)
    hidden = (swish_pre * swish_sig * linear_pre).astype(BF16)
    down_rows = product(hidden, w_down)
    zero_sig_second = jax.nn.sigmoid(product(cond_low, w_zero_two) + bias_zero_two.astype(F32))
    layer_out = (middle + zero_sig_second * down_rows).astype(BF16)

    upstream = cotangent.reshape(total, width).astype(F32)
    d_down = (upstream * zero_sig_second).astype(BF16)
    d_zero_second = (upstream * down_rows * sigmoid_slope(zero_sig_second)).astype(BF16)
    d_hidden = back_product(d_down, w_down)
    d_swish = (
        d_hidden * linear_pre * swish_sig * (1.0 + swish_pre * (1.0 - swish_sig))
    ).astype(BF16)
    d_linear = (d_hidden * swish_pre * swish_sig).astype(BF16)
    d_adapted_two = back_product(d_swish, w_swish) + back_product(d_linear, w_linear)
    d_shift_second = d_adapted_two.astype(BF16)
    d_pre_second = (d_adapted_two * mid_normed * sigmoid_slope(sig_second)).astype(BF16)
    d_cond_second = back_product(d_shift_second, w_shift_two) + back_product(
        d_pre_second, w_scale_two
    )
    d_middle = upstream + norm_back(mid_normed, mid_inverse, d_adapted_two * sig_second)
    d_branch = (d_middle * zero_sig_first).astype(BF16)
    d_zero_first = (d_middle * branch * sigmoid_slope(zero_sig_first)).astype(BF16)
    d_gated = back_product(d_branch, w_out)
    d_gate = (d_gated * attn_float * sigmoid_slope(gate_sig)).astype(BF16)
    d_attended = (d_gated * gate_sig).astype(BF16)

    late_grads = (
        outer_sum(gated_rows, d_branch),
        outer_sum(cond_low, d_zero_first),
        outer_sum(cond_second, d_pre_second),
        outer_sum(cond_second, d_shift_second),
        outer_sum(adapted_two, d_swish),
        outer_sum(adapted_two, d_linear),
        outer_sum(hidden, d_down),
        outer_sum(cond_low, d_zero_second),
    )

    d_query, d_key, d_value, bias_grad = attend_back(
        struct_of, structs, query_split, key_value[0], key_value[1],
        d_attended.reshape(samples, rows, width), prob,
    )
    d_key_value = lax.psum_scatter(
        jnp.stack((d_key, d_value)), "head", scatter_dimension=2, tiled=True
    )
    d_query = d_query.reshape(total, width)
    d_key = d_key_value[0].reshape(total, width)
    d_value = d_key_value[1].reshape(total, width)
    bias_summed = lax.psum_scatter(bias_grad, "samp", scatter_dimension=3, tiled=True)
    pair_weight_grad = jnp.einsum("sijc,shij->ch", pair_low, bias_summed, preferred_element_type=F32)
    pair_upstream = jnp.einsum(
        "shij,ch->sijc", bias_summed, pair_proj_w, preferred_element_type=F32
    )
    pair_grad = norm_back(pair_normed, pair_inverse, pair_upstream)
    d_adapted = (
        back_product(d_query, w_query)
        + back_product(d_key, w_key)
        + back_product(d_value, w_value)
        + back_product(d_gate, w_gate)
    )
    d_shift_first = d_adapted.astype(BF16)
    d_pre_first = (d_adapted * act_normed * sigmoid_slope(sig_first)).astype(BF16)
    d_cond_first = back_product(d_shift_first, w_shift) + back_product(d_pre_first, w_scale)
    input_grad = d_middle + norm_back(act_normed, act_inverse, d_adapted * sig_first)
    d_cond_normed = d_cond_first * gain_one.astype(F32) + d_cond_second * gain_two.astype(F32)
    cond_grad = (
        norm_back(cond_normed, cond_inverse, d_cond_normed)
        + back_product(d_zero_first, w_zero)
        + back_product(d_zero_second, w_zero_two)
    )
    early_grads = (
        outer_sum(cond_first, d_pre_first),
        outer_sum(cond_first, d_shift_first),
        outer_sum(adapted, d_query),
        outer_sum(adapted, d_key),
        outer_sum(adapted, d_value),
        outer_sum(adapted, d_gate),
    )
    small_grads = (
        jnp.sum(d_cond_first * cond_normed, axis=0),
        column_sum(d_pre_first),
        column_sum(d_query),
        column_sum(d_zero_first),
        jnp.sum(d_cond_second * cond_normed, axis=0),
        column_sum(d_pre_second),
        column_sum(d_zero_second),
        pair_weight_grad,
    )
    count = lax.axis_size("samp")

    def pack_grads(grads, shapes):
        pieces = [
            grad.astype(BF16).reshape(count, shape[0] * shape[1] // width, width)
            for grad, shape in zip(grads, shapes)
        ]
        return jnp.concatenate(pieces, axis=1)

    def reduce(packed):
        summed = lax.psum_scatter(packed, "samp", scatter_dimension=0, tiled=True)
        return lax.psum(summed[0], "head").astype(F32)

    late_sum = reduce(pack_grads(late_grads, [piece.shape for piece in late]))
    early_sum = reduce(pack_grads(early_grads, [piece.shape for piece in early]))
    small_flat = jnp.concatenate(
        [grad.astype(BF16).reshape(count, -1) for grad in small_grads], axis=1
    )
    small_sum = lax.psum(
        lax.psum_scatter(small_flat, "samp", scatter_dimension=0, tiled=True), "head"
    ).astype(F32)
    (g_out, g_zero, g_scale_two, g_shift_two, g_swish, g_linear, g_down, g_zero_two) = unpack_rows(
        late_sum[None], [piece.shape for piece in late]
    )
    (g_scale, g_shift, g_query, g_key, g_value, g_gate) = unpack_rows(
        early_sum[None], [piece.shape for piece in early]
    )
    (g_gain, g_bias, g_bias_query, g_bias_zero, g_gain_two, g_bias_two, g_bias_zero_two, g_pair) = (
        unpack_small(small_sum, [piece.shape for piece in small])
    )
    return (
        layer_out.reshape(act.shape), input_grad.reshape(act.shape), cond_grad.reshape(cond.shape),
        pair_grad, g_gain, g_scale, g_bias, g_shift, g_query, g_bias_query, g_key, g_value, g_gate,
        g_out, g_pair, g_zero, g_bias_zero, g_gain_two, g_scale_two, g_bias_two, g_shift_two,
        g_swish, g_linear, g_down, g_zero_two, g_bias_zero_two,
    )


def solution(mesh):
    tokens = P("samp", "head", None)
    pairs = P(None, "head", "samp", None)
    vector = P("samp")
    matrix = P("samp", None)
    weights = (
        vector, matrix, vector, matrix, matrix, vector, matrix, matrix, matrix, matrix, matrix,
        matrix, vector, vector, matrix, vector, matrix, matrix, matrix, matrix, matrix, vector,
    )
    return jax.shard_map(
        per_device,
        mesh=mesh,
        in_specs=(tokens, tokens, pairs, vector, P()) + weights + (tokens,),
        out_specs=(tokens, tokens, tokens, pairs) + weights,
        check_vma=False,
    )
```

profile of v0, /device:TPU:0, one launch (start us, length us, event | category | flops | bytes accessed | tf_op | source)
XLA Modules:
  0.0 806.8 jit_solution(14891443416695150102)
XLA Ops:
  19.2 10.9 %all_gather.23 = bf16[8,8,768]{2,1,0:T(8,128)(2,1)S(1)} all-gather(bf16[1,8,768]{2,1,0:T(8,128)(2,1)S(1)} %all_gather_reshape.3), channel_id=1, replica_groups=mesh['samp'=8,'head'=4] {'samp'}, dimensions={0}, use_global_device_ids=true | all-gather | bytes 110592 | tf_op jit(solution)/shard_map/all_gather | solution.py:285
  30.3 10.1 %convert_reduce_fusion = f32[3,136,68]{2,1,0:T(8,128)S(1)} fusion(bf16[3,136,68,128]{3,1,2,0:T(8,128)(2,1)} %param.30), kind=kLoop, calls=%fused_computation.1 | loop fusion | flops 7074720 | bytes 7213440 | tf_op jit(solution)/shard_map/reduce_sum | solution.py:19
  40.5 13.0 %fusion.8 = f32[3,136,68]{2,1,0:T(8,128)S(1)} fusion(f32[3,136,68]{2,1,0:T(8,128)S(1)} %broadcast_multiply_fusion.2, bf16[3,136,68,128]{3,1,2,0:T(8,128)(2,1)S(1)} %copy-done.7), kind=kLoop, calls=%fused_computation.10 | loop fusion | flops 14177184 | bytes 7324416 | tf_op jit(solution)/shard_map/reduce_sum | solution.py:20
  54.3 14.5 %fusion.14 = bf16[3,16,136,68]{3,1,2,0:T(8,128)(2,1)S(1)} fusion(bf16[128,16]{1,0:T(8,128)(2,1)S(1)} %reshape.529, f32[3,136,68]{2,1,0:T(8,128)S(1)} %add_rsqrt_fusion, f32[3,136,68]{2,1,0:T(8,128)S(1)} %broadcast_multiply_fusion.2, bf16[3,136,68,128]{3,1,2,0:T(8,128)(2,1)S(1)} %copy-done.7), kind=kOutput, calls=%fused_computation.33 | convolution fusion | flops 128288256 | bytes 8216320 | tf_op jit(solution)/shard_map/sijc,ch->shij/dot_general | solution.py:300
  101.9 47.1 %all-gather.9.cloned.1.call-done = bf16[3,16,136,544]{2,1,0,3:T(8,128)(2,1)} async-done(((bf16[3,16,136,68]{2,1,0,3:T(8,128)(2,1)}), bf16[3,16,136,544]{2,1,0,3:T(8,128)(2,1)}) %all-gather.9.cloned.1.call-update) | async-done | bytes 7102480 | tf_op jit(solution)/shard_map/all_gather | solution.py:301
  149.0 18.5 %copy.81.bias_ref = bf16[3,16,136,544]{3,2,1,0:T(8,128)(2,1)} copy(bf16[3,16,136,544]{2,1,0,3:T(8,128)(2,1)} %all-gather.9.cloned.1.call-done) | data formatting | bytes 14204928 | tf_op jit(solution)/shard_map/all_gather | solution.py:301
  167.5 50.4 %all-gather.7.cloned.1.call-done = bf16[2,2,544,768]{3,2,1,0:T(8,128)(2,1)} async-done(((bf16[2,2,136,768]{3,2,1,0:T(8,128)(2,1)}), bf16[2,2,544,768]{3,2,1,0:T(8,128)(2,1)}) %all-gather.7.cloned.1.call-update) | async-done | bytes 3342352 | tf_op jit(solution)/shard_map/all_gather | solution.py:315
  220.2 16.1 %attend.1 = (bf16[2,136,768]{2,1,0:T(8,128)(2,1)S(1)}, bf16[2,16,136,544]{3,2,1,0:T(8,128)(2,1)}) custom-call(s32[2]{0:T(128)S(1)} %copy-done.5, s32[3]{0:T(128)S(1)} %copy-done.6, bf16[2,136,768]{2,1,0:T(8,128)(2,1)S(1)} %bitcast.217, bf16[2,544,768]{2,1,0:T(8,128)(2,1)S(1)} %get-tuple-element.189.k_ref, bf16[2,544,768]{2,1,0:T(8,128)(2,1)S(1)} %get-tuple-element.188.v_ref, ...), custom_call_target="tpu_custom_call" | custom-call | tf_op jit(solution)/shard_map/attend/pallas_call | solution.py:119
  238.7 43.5 %all-gather.11.cloned.1.call-done = bf16[6912,768]{1,0:T(8,128)(2,1)} async-done(((bf16[864,768]{1,0:T(8,128)(2,1)}), bf16[6912,768]{1,0:T(8,128)(2,1)}) %all-gather.11.cloned.1.call-update) | async-done | bytes 10616848 | tf_op jit(solution)/shard_map/all_gather | solution.py:287
  286.8 6.7 fusion.90
  324.3 20.2 %attend_back.1 = (bf16[2,136,768]{2,1,0:T(8,128)(2,1)}, bf16[2,544,768]{2,1,0:T(8,128)(2,1)}, bf16[2,544,768]{2,1,0:T(8,128)(2,1)}, bf16[3,16,136,544]{3,2,1,0:T(8,128)(2,1)}) custom-call(s32[2]{0:T(128)} %struct_ref.3, bf16[2,136,768]{2,1,0:T(8,128)(2,1)} %bitcast.216, bf16[2,544,768]{2,1,0:T(8,128)(2,1)} %copy-done.1, bf16[2,544,768]{2,1,0:T(8,128)(2,1)} %copy-done, ...), custom_call_target="tpu_custom_call" | custom-call | tf_op jit(solution)/shard_map/attend_back/pallas_call | solution.py:193
  346.8 5.1 copy.123
  352.0 8.4 %reshape.601 = bf16[544,3072]{1,0:T(8,128)(2,1)} reshape(bf16[544,2,2,768]{3,2,1,0:T(2,128)(2,1)} %bitcast.223) | data formatting | bytes 6684672
  369.5 54.4 %reduce-scatter.11.cloned.1.call-done = bf16[136,3072]{1,0:T(8,128)(2,1)} async-done(((bf16[544,3072]{1,0:T(8,128)(2,1)}), bf16[136,3072]{1,0:T(8,128)(2,1)}) %reduce-scatter.11.cloned.1.call-update) | async-done | bytes 835600
  449.1 5.3 reshape.568
  457.3 4.8 reshape.567
  479.2 75.6 %all-reduce.7.cloned.1.call-done = bf16[3,16,136,544]{3,2,1,0:T(8,128)(2,1)} async-done(((bf16[3,16,136,544]{3,2,1,0:T(8,128)(2,1)}), bf16[3,16,136,544]{3,2,1,0:T(8,128)(2,1)}) %all-reduce.7.cloned.1.call-update) | async-done | bytes 7102480
  557.6 31.8 %fusion.77 = (f32[3,136,68]{2,1,0:T(8,128)S(1)}, f32[3,136,68]{2,1,0:T(8,128)S(1)}, f32[3,136,68,128]{3,2,1,0:T(8,128)S(1)}) fusion(f32[3,136,68]{2,1,0:T(8,128)S(1)} %copy-done.61, f32[3,136,68]{2,1,0:T(8,128)S(1)} %copy-done.48, bf16[3,136,68,128]{3,1,2,0:T(8,128)(2,1)} %param.30, bf16[128,16]{1,0:T(8,128)(2,1)S(1)} %copy-done.77, ...), kind=kOutput, calls=%fused_computation.216 | convolution fusion | flops 134891328 | bytes 22643200 | tf_op jit(solution)/shard_map/shij,ch->sijc/dot_general | solution.py:382
  589.4 28.3 %fusion.4 = (bf16[3,136,68,128]{3,2,1,0:T(8,128)(2,1)S(1)}, f32[3,136,68,128]{3,2,1,0:T(8,128)}) fusion(f32[3,136,68]{2,1,0:T(8,128)S(1)} %copy-done.61, f32[3,136,68]{2,1,0:T(8,128)S(1)} %copy-done.48, bf16[3,136,68,128]{3,1,2,0:T(8,128)(2,1)S(1)} %bitcast.219, f32[3,136,68]{2,1,0:T(8,128)S(1)} %broadcast_multiply_fusion, ...), kind=kLoop, calls=%fused_computation.6 | loop fusion | flops 28409856 | bytes 43058688 | tf_op jit(solution)/shard_map/convert_element_type | solution.py:299
  619.3 15.1 %copy.87 = f32[3,136,68,128]{3,1,2,0:T(8,128)} copy(f32[3,136,68,128]{3,2,1,0:T(8,128)} %get-tuple-element.178) | data formatting | bytes 28409856
  634.8 22.8 %all-reduce.2 = bf16[8,832]{1,0:T(8,128)(2,1)S(1)} all-reduce(bf16[8,832]{1,0:T(8,128)(2,1)S(1)} %concatenate.22), channel_id=6, replica_groups=mesh['samp'=8,'head'=4] {'samp'}, use_global_device_ids=true, to_apply=%region_25.26.clone | all-reduce | flops 6656 | bytes 26624
  658.2 11.7 %psum.21 = bf16[1,832]{1,0:T(2,128)(2,1)S(1)} all-reduce(bf16[1,832]{1,0:T(2,128)(2,1)S(1)} %constant_dynamic-slice_fusion), channel_id=1, replica_groups=mesh['samp'=8,'head'=4] {'head'}, use_global_device_ids=true, to_apply=%region_26.27 | all-reduce | flops 832 | bytes 3328 | tf_op jit(solution)/shard_map/psum | solution.py:438
  670.5 33.5 %reduce-scatter.9.cloned.1.call-done = bf16[1,864,768]{2,1,0:T(8,128)(2,1)} async-done(((bf16[8,864,768]{2,1,0:T(8,128)(2,1)}), bf16[1,864,768]{2,1,0:T(8,128)(2,1)}) %reduce-scatter.9.cloned.1.call-update) | async-done | bytes 1327120 | tf_op jit(solution)/shard_map/reduce_scatter | solution.py:430
  710.2 82.1 %all-reduce.9.cloned.1.call-done = (bf16[1,480,768]{2,1,0:T(8,128)(2,1)}, bf16[1,864,768]{2,1,0:T(8,128)(2,1)}) async-done(((bf16[1,480,768]{2,1,0:T(8,128)(2,1)}, bf16[1,864,768]{2,1,0:T(8,128)(2,1)}), (bf16[1,480,768]{2,1,0:T(8,128)(2,1)}, bf16[1,864,768]{2,1,0:T(8,128)(2,1)})) %all-reduce.9.cloned.1.call-update) | async-done | bytes 2064400 | tf_op jit(solution)/shard_map/psum | solution.py:431
  (392 shorter events, 160.6 us)
Async XLA Ops:
  7.2 68.3 %all-gather.13.cloned.1.call-start = ((), (), s32[]{:S(2)}) async-start(), calls=%async_computation.8 | async-start | bytes 6635520 | tf_op jit(solution)/shard_map/all_gather | solution.py:286
  13.6 135.4 %all-gather.9.cloned.1.call-start = ((), (), s32[]{:S(2)}) async-start(), calls=%async_computation.4 | async-start | bytes 15040512 | tf_op jit(solution)/shard_map/all_gather | solution.py:301
  30.3 23.3 %copy-start.76 = (bf16[128,16]{1,0:T(8,128)(2,1)}, bf16[128,16]{1,0:T(8,128)(2,1)S(1)}, u32[]{:S(2)}) copy-start(bf16[128,16]{1,0:T(8,128)(2,1)S(1)} %reshape.529) | copy-start | bytes 12292
  73.1 144.8 %all-gather.7.cloned.1.call-start = ((), (), s32[]{:S(2)}) async-start(), calls=%async_computation.3 | async-start | bytes 4177920 | tf_op jit(solution)/shard_map/all_gather | solution.py:315
  80.4 155.9 %copy-start.31 = (bf16[272,768]{1,0:T(8,128)(2,1)}, bf16[272,768]{1,0:T(8,128)(2,1)S(1)}, u32[]{:S(2)}) copy-start(bf16[272,768]{1,0:T(8,128)(2,1)S(1)} %fusion.37) | copy-start | bytes 1253380
  84.4 197.8 %all-gather.11.cloned.1.call-start = ((), (), s32[]{:S(2)}) async-start(), calls=%async_computation.7 | async-start | bytes 11943936 | tf_op jit(solution)/shard_map/all_gather | solution.py:287
  99.8 324.1 %reduce-scatter.11.cloned.1.call-start = ((), (), s32[]{:S(2)}) async-start(), calls=%async_computation.9 | async-start | bytes 4177920
  167.5 52.7 %copy-start.5 = (s32[2]{0:T(128)S(1)}, s32[2]{0:T(128)}, u32[]{:S(2)}) copy-start(s32[2]{0:T(128)} %struct_ref.3) | copy-start | bytes 28
  167.5 52.7 %copy-start.6 = (s32[3]{0:T(128)S(1)}, s32[3]{0:T(128)}, u32[]{:S(2)}) copy-start(s32[3]{0:T(128)} %len_ref.1) | copy-start | bytes 40
  286.7 20.0 %copy-start.22 = (bf16[8,48,768]{2,1,0:T(8,128)(2,1)}, bf16[8,48,768]{2,1,0:T(8,128)(2,1)S(1)}, u32[]{:S(2)}) copy-start(bf16[8,48,768]{2,1,0:T(8,128)(2,1)S(1)} %get-tuple-element.174) | copy-start | bytes 1769476
  321.1 23.5 %copy-start.52 = (bf16[272,768]{1,0:T(8,128)(2,1)}, bf16[272,768]{1,0:T(8,128)(2,1)S(1)}, u32[]{:S(2)}) copy-start(bf16[272,768]{1,0:T(8,128)(2,1)S(1)} %multiply_convert_fusion.4) | copy-start | bytes 1253380
  360.5 194.4 %all-reduce.7.cloned.1.call-start = ((), (), s32[]{:S(2)}) async-start(), calls=%async_computation.10 | async-start | bytes 16711680
  369.5 301.1 %reduce-scatter.7.cloned.1.call-start = ((), (), s32[]{:S(2)}) async-start(), calls=%async_computation.5 | async-start | bytes 6635520 | tf_op jit(solution)/shard_map/reduce_scatter | solution.py:430
  445.0 259.0 %reduce-scatter.9.cloned.1.call-start = ((), (), s32[]{:S(2)}) async-start(), calls=%async_computation.6 | async-start | bytes 11943936 | tf_op jit(solution)/shard_map/reduce_scatter | solution.py:430
  476.9 80.6 %copy-start.48 = (f32[3,136,68]{2,1,0:T(8,128)S(1)}, f32[3,136,68]{2,1,0:T(8,128)}, u32[]{:S(2)}) copy-start(f32[3,136,68]{2,1,0:T(8,128)} %copy-done.47) | copy-start | bytes 332932
  477.0 80.6 %copy-start.61 = (f32[3,136,68]{2,1,0:T(8,128)S(1)}, f32[3,136,68]{2,1,0:T(8,128)}, u32[]{:S(2)}) copy-start(f32[3,136,68]{2,1,0:T(8,128)} %copy-done.60) | copy-start | bytes 332932
  477.0 80.6 %copy-start.77 = (bf16[128,16]{1,0:T(8,128)(2,1)S(1)}, bf16[128,16]{1,0:T(8,128)(2,1)}, u32[]{:S(2)}) copy-start(bf16[128,16]{1,0:T(8,128)(2,1)} %copy-done.76) | copy-start | bytes 12292
  477.0 315.3 %all-reduce.9.cloned.1.call-start = ((), (), s32[]{:S(2)}) async-start(), calls=%async_computation.11 | async-start | bytes 4128768 | tf_op jit(solution)/shard_map/psum | solution.py:431
  554.9 34.6 %slice-start = ((s8[7102464]{0:T(1024)(128)(4,1)}), s8[4194304]{0:T(1024)(128)(4,1)S(1)}, s32[]{:S(2)}) async-start(s8[7102464]{0:T(1024)(128)(4,1)} %bitcast.218), calls=%async_computation.12 | async-start | bytes 8388608
  557.6 31.9 %slice-start.1 = ((s8[7102464]{0:T(1024)(128)(4,1)}), s8[2908160]{0:T(1024)(128)(4,1)S(1)}, s32[]{:S(2)}) async-start(s8[7102464]{0:T(1024)(128)(4,1)} %bitcast.218), calls=%async_computation.13 | async-start | bytes 5816320
  619.2 86.2 %copy-start.89 = (f32[272]{0:T(512)S(1)}, f32[272]{0:T(512)}, u32[]{:S(2)}) copy-start(f32[272]{0:T(512)} %get-tuple-element.148) | copy-start | bytes 3268
  619.2 86.2 %copy-start.87 = (f32[272]{0:T(512)S(1)}, f32[272]{0:T(512)}, u32[]{:S(2)}) copy-start(f32[272]{0:T(512)} %get-tuple-element.144) | copy-start | bytes 3268
  619.3 86.2 %copy-start.86 = (f32[272]{0:T(512)S(1)}, f32[272]{0:T(512)}, u32[]{:S(2)}) copy-start(f32[272]{0:T(512)} %get-tuple-element.145) | copy-start | bytes 3268
  619.3 86.2 %copy-start.88 = (f32[272]{0:T(512)S(1)}, f32[272]{0:T(512)}, u32[]{:S(2)}) copy-start(f32[272]{0:T(512)} %get-tuple-element.149) | copy-start | bytes 3268
  (90 other events, 333.7 us)
Sparse Core Ops, SparseCore 0:
  13.7 46.7 all-gather.12
  73.2 75.7 all-gather.8
  151.2 66.6 all-gather.6
  219.7 62.4 all-gather.10
  360.6 63.3 reduce-scatter.10
  428.2 126.5 all-reduce.6
  558.3 59.7 reduce-scatter.6
  621.6 82.3 reduce-scatter.8
  706.5 85.7 all-reduce.8
where the time goes:
time: 818 us; the launch traced here: 807 us
  waiting for transfers between devices  387 us (47%)
  local copies, waits for them, and re-layouts  166 us (20%)
  matrix products  91.5 us (11%)
  other arithmetic  63.9 us (8%)
  blocking collectives  45.4 us (6%)
  Pallas kernels  36.4 us (4%)
  between operations  16 us (2%)
    unnamed x11, waiting for transfers between devices  130 us
    psum x1, waiting for transfers between devices, reduce(): return lax.psum(summed[0], 'head').astype(F32)  82.1 us
    unnamed x244, local copies, waits for them, and re-layouts  80.8 us
    all_gather x1, waiting for transfers between devices, per_device(): key_value = lax.all_gather(key_value, 'head', axis=2, tiled=True)  50.4 us
    all_gather x1, waiting for transfers between devices, per_device(): lax.all_gather(pair_proj.astype(BF16), 'samp', axis=3, tiled=True)  47.1 us
    all_gather x1, waiting for transfers between devices, per_device(): late_all = lax.all_gather(pack_rows(late, width), 'samp', axis=0)  43.5 us
    reduce_scatter x2, waiting for transfers between devices, reduce(): summed = lax.psum_scatter(packed, 'samp', scatter_dimension=0, tiled=True)  33.5 us
    dot_general x1, matrix products, per_device(): jnp.einsum('shij,ch->sijc', bias_summed, pair_proj_w, preferred_element_t...  31.8 us
  transfers between devices with their start and end apart: 9, of which 7 were waited for; matrix products, arithmetic and copies ran while one was open for 30% of the time, Pallas kernels for 2%

commit v1 on v0

--- a/solution.py
+++ b/solution.py
@@ -9,6 +9,9 @@
 
 HEAD_DIM = 48
 LANES = 128
+MAIN = 64
+KEY_LANES = 640
+MESH = pl.DeviceIdType.MESH
 EPSILON = 1e-05
 NEG_BIG = -1000000000.0
 F32 = jnp.float32
@@ -84,7 +87,480 @@
     return lax.dot_general(left, right, (((0,), (0,)), ((), ())), preferred_element_type=F32)
 
 
-def attend_kernel(struct_ref, len_ref, q_ref, k_ref, v_ref, bias_ref, out_ref, prob_ref, acc_ref):
+def key_rows_order(rows, block):
+    pieces = rows.shape[1] // block
+    main = [rows[:, at * block : at * block + MAIN] for at in range(pieces)]
+    tail = [rows[:, at * block + MAIN : (at + 1) * block] for at in range(pieces)]
+    return jnp.concatenate(main + tail, axis=1)
+
+
+def key_rows_back(rows, block):
+    pieces = rows.shape[1] // block
+    tail = block - MAIN
+    parts = []
+    for at in range(pieces):
+        parts.append(rows[:, at * MAIN : (at + 1) * MAIN])
+        parts.append(rows[:, pieces * MAIN + at * tail : pieces * MAIN + (at + 1) * tail])
+    return jnp.concatenate(parts, axis=1)
+
+
+def pack_bias(bias):
+    structs, heads, rows, block = bias.shape
+    main = bias[..., :MAIN].reshape(structs, heads // 2, 2, rows, MAIN)
+    main = main.transpose(0, 1, 3, 2, 4).reshape(-1, rows, LANES)
+    tail = bias[..., MAIN:].transpose(0, 2, 1, 3).reshape(structs, rows, -1)
+    tail = jnp.pad(tail, ((0, 0), (0, 0), (0, LANES - tail.shape[2])))
+    return jnp.concatenate((main, tail), axis=0)
+
+
+def unpack_bias(packed, structs, heads):
+    rows = packed.shape[1]
+    pairs = structs * heads // 2
+    main = packed[:pairs].reshape(structs, heads // 2, rows, 2, MAIN)
+    main = main.transpose(0, 1, 3, 2, 4).reshape(structs, heads, rows, MAIN)
+    tail = packed[pairs:, :, :MAIN].reshape(structs, rows, heads, -1).transpose(0, 2, 1, 3)
+    return jnp.concatenate((main, tail), axis=3)
+
+
+def tail_switch(count, heads, tail):
+    lanes = count * heads * tail
+    source = lax.broadcasted_iota(jnp.int32, (lanes, lanes), 0)
+    target = lax.broadcasted_iota(jnp.int32, (lanes, lanes), 1)
+    owner = source // (heads * tail)
+    head = source // tail % heads
+    spot = head * (count * tail) + owner * tail + source % tail
+    return jnp.where(spot == target, 1.0, 0.0).astype(BF16)
+
+
+def swap_halves(tile):
+    return pltpu.roll(tile, MAIN, 1)
+
+
+def low_half(tile):
+    return lax.broadcasted_iota(jnp.int32, tile.shape, 1) < MAIN
+
+
+def key_places(count, block):
+    lane = lax.broadcasted_iota(jnp.int32, (1, KEY_LANES), 1)
+    tail = block - MAIN
+    spare = lane - count * MAIN
+    main_at = lane + tail * (lane // MAIN)
+    tail_at = block * (spare // tail) + MAIN + spare % tail
+    past = jnp.where(spare < count * tail, tail_at, count * block)
+    return jnp.where(spare < 0, main_at, past)
+
+
+def attend_kernel(
+    struct_ref, len_ref, q_ref, kv_ref, pack_ref, out_ref, prob_ref, key_ref, value_ref, tail_ref, acc_ref
+):
+    samples, rows, width = q_ref.shape
+    count = pack_ref.shape[0]
+    spans = kv_ref.shape[0]
+    heads = width // HEAD_DIM
+    block = rows * spans // count
+    tail = block - MAIN
+    structs = pack_ref.shape[1] // (heads // 2 + 1)
+    main_rows = rows // block * MAIN
+    keys = count * block
+    group, windows = head_windows(width)
+    switch = tail_switch(count, heads, tail)
+    places = key_places(count, block)
+    key_ref[keys:] = jnp.zeros_like(key_ref[keys:])
+    value_ref[keys:] = jnp.zeros_like(value_ref[keys:])
+
+    def one_sample(sample, carry):
+        struct = struct_ref[sample]
+        valid = places < len_ref[struct]
+        for span in range(spans):
+            for which, held in ((0, key_ref), (1, value_ref)):
+                held[span * main_rows : (span + 1) * main_rows] = kv_ref[span, which, sample, :main_rows]
+                spot = count * MAIN + span * (rows - main_rows)
+                held[spot : spot + rows - main_rows] = kv_ref[span, which, sample, main_rows:]
+        tiles = []
+        for pair in range(count // 2):
+            even = pack_ref[2 * pair, structs * heads // 2 + struct]
+            odd = swap_halves(pack_ref[2 * pair + 1, structs * heads // 2 + struct])
+            tiles.append(jnp.where(low_half(even), even, odd))
+        mixed = dot_nn(jnp.concatenate(tiles, axis=1), switch).astype(BF16)
+        for at in range(count // 2):
+            tail_ref[at] = mixed[:, at * LANES : (at + 1) * LANES]
+
+        def one_group(place, carry):
+            acc_ref[...] = jnp.zeros_like(acc_ref)
+            for at, (start, span, offset) in enumerate(windows):
+                lanes = pl.ds(pl.multiple_of(place * group + start, LANES), span)
+                mask = head_mask(span, offset)
+                tile = struct * (heads // 2) + place * (len(windows) // 2) + at // 2
+                bias = []
+                for pair in range(count // 2):
+                    even = pack_ref[2 * pair, tile]
+                    odd = pack_ref[2 * pair + 1, tile]
+                    if at % 2 == 0:
+                        bias.append(jnp.where(low_half(even), even, swap_halves(odd)))
+                    else:
+                        bias.append(jnp.where(low_half(even), swap_halves(even), odd))
+                per_tile = LANES // (count * tail)
+                rest = tail_ref[place * (len(windows) // per_tile) + at // per_tile]
+                turn = at % per_tile * count * tail
+                bias.append(pltpu.roll(rest, LANES - turn, 1) if turn else rest)
+                query = q_ref[sample, :, lanes]
+                query = jnp.where(mask, query, jnp.zeros_like(query))
+                scores = dot_nt(query, key_ref[:, lanes]) * HEAD_DIM ** (-0.5) + jnp.concatenate(
+                    bias, axis=1
+                ).astype(F32)
+                scores = jnp.where(valid, scores, NEG_BIG)
+                weights = jnp.exp(scores - jnp.max(scores, axis=1, keepdims=True))
+                weights = weights * (1.0 / jnp.sum(weights, axis=1, keepdims=True))
+                weights = weights.astype(BF16)
+                prob_ref[sample, place * len(windows) + at] = weights
+                mixed = dot_nn(weights, value_ref[:, lanes])
+                within = slice(start, start + span)
+                acc_ref[:, within] += jnp.where(mask, mixed, 0.0)
+            out_ref[sample, :, pl.ds(pl.multiple_of(place * group, LANES), group)] = acc_ref[
+                ...
+            ].astype(BF16)
+            return carry
+
+        return lax.fori_loop(0, width // group, one_group, carry)
+
+    lax.fori_loop(0, samples, one_sample, 0)
+
+
+def attend(struct_of, struct_len, query, key_value, packed):
+    samples, rows, width = query.shape
+    group, windows = head_windows(width)
+    count = packed.shape[0]
+    heads = width // HEAD_DIM
+    vmem = pl.BlockSpec(memory_space=pltpu.VMEM)
+    smem = pl.BlockSpec(memory_space=pltpu.SMEM)
+    return pl.pallas_call(
+        attend_kernel,
+        out_shape=(
+            jax.ShapeDtypeStruct((samples, rows, width), BF16),
+            jax.ShapeDtypeStruct((samples, heads, rows, KEY_LANES), BF16),
+        ),
+        in_specs=[smem, smem, vmem, vmem, vmem],
+        out_specs=[vmem, vmem],
+        scratch_shapes=[
+            pltpu.VMEM((KEY_LANES, width), BF16),
+            pltpu.VMEM((KEY_LANES, width), BF16),
+            pltpu.VMEM((count // 2, rows, LANES), BF16),
+            pltpu.VMEM((rows, group), F32),
+        ],
+        compiler_params=pltpu.CompilerParams(vmem_limit_bytes=56 << 20),
+        name="attend",
+    )(struct_of, struct_len, query, key_value, packed)
+
+
+def flip(index, bit):
+    return index + bit - 2 * bit * lax.rem(lax.div(index, bit), 2)
+
+
+def flips(index, bits):
+    spots = [index]
+    for bit in bits:
+        spots = spots + [flip(spot, bit) for spot in spots]
+    return spots
+
+
+def reduce_orders(count):
+    bits = []
+    bit = 2
+    while bit < count:
+        bits.append(bit)
+        bit *= 2
+    half = len(bits) // 2
+    return ([1] + bits, [1] + bits[half:] + bits[:half])
+
+
+def greet(partners):
+    barrier = pltpu.get_barrier_semaphore()
+    for partner in partners:
+        pl.semaphore_signal(barrier, inc=1, device_id=partner, device_id_type=MESH)
+    pl.semaphore_wait(barrier, len(partners))
+
+
+def send(source, target, send_sem, recv_sem, device):
+    return pltpu.make_async_remote_copy(
+        src_ref=source, dst_ref=target, send_sem=send_sem, recv_sem=recv_sem,
+        device_id=device, device_id_type=MESH,
+    )
+
+
+def attend_back_kernel(
+    struct_ref, q_ref, kv_ref, do_ref, prob_ref, dq_ref, dkv_ref, dpb_ref,
+    key_ref, value_ref, dq_acc, dk_acc, dv_acc, first_ref, tail_ref, part_ref, span_ref, pack_ref,
+    got_zero, got_one, got_two, span_send, span_recv, pack_send, pack_recv,
+):
+    samples, rows, width = q_ref.shape
+    count = pack_ref.shape[0]
+    spans = kv_ref.shape[0]
+    heads = width // HEAD_DIM
+    block = rows * spans // count
+    tail = block - MAIN
+    structs = pack_ref.shape[1] // (heads // 2 + 1)
+    main_rows = rows // block * MAIN
+    keys = count * block
+    group, windows = head_windows(width)
+    scale = HEAD_DIM ** (-0.5)
+    me = lax.axis_index("samp")
+    my_span = lax.axis_index("head")
+    orders = reduce_orders(count)
+    others = [lax.rem(my_span + away, spans) for away in range(1, spans)]
+    greet(
+        [dict(samp=flip(me, bit)) for bit in sorted(orders[0])] + [dict(head=other) for other in others]
+    )
+    switch = tail_switch(count, heads, tail)
+    key_ref[keys:] = jnp.zeros_like(key_ref[keys:])
+    value_ref[keys:] = jnp.zeros_like(value_ref[keys:])
+
+    def span_copy(place, sample, away):
+        lanes = pl.ds(pl.multiple_of(place * group, LANES), group)
+        return send(
+            part_ref.at[others[away], :, sample, :, lanes],
+            span_ref.at[away, :, sample, :, lanes],
+            span_send.at[place, sample, away],
+            span_recv.at[place, sample, away],
+            dict(head=others[away]),
+        )
+
+    def one_group(place, carry):
+        for sample in range(samples):
+            for span in range(spans):
+                for which, held in ((0, key_ref), (1, value_ref)):
+                    held[span * main_rows : (span + 1) * main_rows] = kv_ref[
+                        span, which, sample, :main_rows, pl.ds(pl.multiple_of(place * group, LANES), group)
+                    ]
+                    spot = count * MAIN + span * (rows - main_rows)
+                    held[spot : spot + rows - main_rows] = kv_ref[
+                        span, which, sample, main_rows:, pl.ds(pl.multiple_of(place * group, LANES), group)
+                    ]
+            dq_acc[...] = jnp.zeros_like(dq_acc)
+            dk_acc[...] = jnp.zeros_like(dk_acc)
+            dv_acc[...] = jnp.zeros_like(dv_acc)
+            kept = [jnp.where(struct_ref[0] == slab, 1.0, 0.0).astype(BF16) for slab in range(structs)]
+            added = [jnp.where(struct_ref[1] == slab, 1.0, 0.0).astype(BF16) for slab in range(structs)]
+            even_scores = None
+            for at, (start, span, offset) in enumerate(windows):
+                lanes = pl.ds(pl.multiple_of(place * group + start, LANES), span)
+                within = slice(start, start + span)
+                mask = head_mask(span, offset)
+                upstream = do_ref[sample, :, lanes]
+                upstream = jnp.where(mask, upstream, jnp.zeros_like(upstream))
+                query = q_ref[sample, :, lanes]
+                query = jnp.where(mask, query, jnp.zeros_like(query))
+                low = prob_ref[sample, place * len(windows) + at]
+                weights = low.astype(F32)
+                d_weights = dot_nt(upstream, value_ref[:, within])
+                dv_acc[:, within] += dot_tn(low[:, :keys], upstream)
+                cross = weights * d_weights
+                delta = jnp.sum(cross, axis=1, keepdims=True)
+                d_scores = (cross - weights * delta).astype(BF16)
+                dq_acc[:, within] += jnp.where(mask, dot_nn(d_scores, key_ref[:, within]), 0.0)
+                dk_acc[:, within] += dot_tn(d_scores[:, :keys], query)
+                per_tile = LANES // (count * tail)
+                turn = at % per_tile * count * tail
+                rest = d_scores[:, count * MAIN :]
+                rest = pltpu.roll(rest, turn, 1) if turn else rest
+                spot = place * (len(windows) // per_tile) + at // per_tile
+                if turn:
+                    tail_ref[sample, spot] += rest
+                else:
+                    tail_ref[sample, spot] = rest
+                if at % 2 == 0:
+                    even_scores = d_scores
+                    continue
+                for pair in range(count // 2):
+                    even = even_scores[:, pair * LANES : (pair + 1) * LANES]
+                    odd = d_scores[:, pair * LANES : (pair + 1) * LANES]
+                    low_tile = jnp.where(low_half(even), even, swap_halves(odd))
+                    high_tile = jnp.where(low_half(even), swap_halves(even), odd)
+                    for side, tile in ((0, low_tile), (1, high_tile)):
+                        owner = 2 * pair + side
+                        if sample == 0:
+                            first_ref[at // 2, owner] = tile
+                            continue
+                        old = first_ref[at // 2, owner]
+                        for slab in range(structs):
+                            spot = slab * (heads // 2) + place * (len(windows) // 2) + at // 2
+                            pack_ref[owner, spot] = old * kept[slab] + tile * added[slab]
+            lanes = pl.ds(pl.multiple_of(place * group, LANES), group)
+            dq_ref[sample, :, lanes] = (dq_acc[...] * scale).astype(BF16)
+            for span in range(spans):
+                spot = count * MAIN + span * (rows - main_rows)
+                for which, total, factor in ((0, dk_acc, scale), (1, dv_acc, 1.0)):
+                    part_ref[span, which, sample, :main_rows, lanes] = (
+                        total[span * main_rows : (span + 1) * main_rows] * factor
+                    ).astype(BF16)
+                    part_ref[span, which, sample, main_rows:, lanes] = (
+                        total[spot : spot + rows - main_rows] * factor
+                    ).astype(BF16)
+            for away in range(spans - 1):
+                span_copy(place, sample, away).start()
+        return carry
+
+    lax.fori_loop(0, width // group, one_group, 0)
+
+    mixed = []
+    for sample in range(samples):
+        whole = jnp.concatenate([tail_ref[sample, at] for at in range(count // 2)], axis=1)
+        mixed.append(dot_nt(whole, switch))
+    for pair in range(count // 2):
+        tiles = [part[:, pair * LANES : (pair + 1) * LANES] for part in mixed]
+        for slab in range(structs):
+            both = jnp.zeros_like(tiles[0])
+            for sample in range(samples):
+                both = both + jnp.where(struct_ref[sample] == slab, tiles[sample], 0.0)
+            spot = structs * heads // 2 + slab
+            pack_ref[2 * pair, spot] = jnp.where(low_half(both), both, 0.0).astype(BF16)
+            pack_ref[2 * pair + 1, spot] = jnp.where(low_half(both), swap_halves(both), 0.0).astype(BF16)
+
+    tiles = pack_ref.shape[1]
+    halves = (pl.ds(0, tiles // 2), pl.ds(tiles // 2, tiles - tiles // 2))
+    bounds = ((0, tiles // 2), (tiles // 2, tiles))
+    landing = (got_zero, got_one, got_two)
+
+    def stage_copies(step, half):
+        order = orders[half]
+        kept = flips(me, order[step + 1 :])
+        return [
+            send(
+                pack_ref.at[flip(spot, order[step]), halves[half]],
+                landing[step].at[at, halves[half]],
+                pack_send.at[step, half, at],
+                pack_recv.at[step, half, at],
+                dict(samp=flip(me, order[step])),
+            )
+            for at, spot in enumerate(kept)
+        ]
+
+    flights = [[stage_copies(step, half) for half in range(2)] for step in range(len(orders[0]))]
+    for half in range(2):
+        for copy in flights[0][half]:
+            copy.start()
+    for step in range(len(orders[0])):
+        for half in range(2):
+            kept = flips(me, orders[half][step + 1 :])
+            for at, spot in enumerate(kept):
+                flights[step][half][at].wait_recv()
+
+                def add(tile, carry, spot=spot, at=at, step=step):
+                    pack_ref[spot, tile] = (
+                        pack_ref[spot, tile].astype(F32) + landing[step][at, tile].astype(F32)
+                    ).astype(BF16)
+                    return carry
+
+                lax.fori_loop(bounds[half][0], bounds[half][1], add, 0)
+            if step + 1 < len(orders[0]):
+                for copy in flights[step + 1][half]:
+                    copy.start()
+
+    def out(tile, carry):
+        dpb_ref[tile] = pack_ref[me, tile]
+        return carry
+
+    lax.fori_loop(0, tiles, out, 0)
+
+    for place in range(width // group):
+        for sample in range(samples):
+            for away in range(spans - 1):
+                span_copy(place, sample, away).wait_recv()
+    for which in range(2):
+        for sample in range(samples):
+            total = part_ref[my_span, which, sample].astype(F32)
+            for away in range(spans - 1):
+                total += span_ref[away, which, sample].astype(F32)
+            dkv_ref[which, sample] = total.astype(BF16)
+    for place in range(width // group):
+        for sample in range(samples):
+            for away in range(spans - 1):
+                span_copy(place, sample, away).wait_send()
+    for stage in flights:
+        for half in stage:
+            for copy in half:
+                copy.wait_send()
+
+
+def attend_back(struct_of, structs, query, key_value, upstream, prob, count):
+    samples, rows, width = query.shape
+    spans = key_value.shape[0]
+    heads = width // HEAD_DIM
+    group, windows = head_windows(width)
+    keys = rows * spans
+    tiles = structs * (heads // 2 + 1)
+    steps = count.bit_length() - 1
+    vmem = pl.BlockSpec(memory_space=pltpu.VMEM)
+    smem = pl.BlockSpec(memory_space=pltpu.SMEM)
+    return pl.pallas_call(
+        attend_back_kernel,
+        out_shape=(
+            jax.ShapeDtypeStruct((samples, rows, width), BF16),
+            jax.ShapeDtypeStruct((2, samples, rows, width), BF16),
+            jax.ShapeDtypeStruct((tiles, rows, LANES), BF16),
+        ),
+        in_specs=[smem, vmem, vmem, vmem, vmem],
+        out_specs=[vmem, vmem, vmem],
+        scratch_shapes=[
+            pltpu.VMEM((KEY_LANES, group), BF16),
+            pltpu.VMEM((KEY_LANES, group), BF16),
+            pltpu.VMEM((rows, group), F32),
+            pltpu.VMEM((keys, group), F32),
+            pltpu.VMEM((keys, group), F32),
+            pltpu.VMEM((len(windows) // 2, count, rows, LANES), BF16),
+            pltpu.VMEM((samples, count // 2, rows, LANES), BF16),
+            pltpu.VMEM((spans, 2, samples, rows, width), BF16),
+            pltpu.VMEM((spans - 1, 2, samples, rows, width), BF16),
+            pltpu.VMEM((count, tiles, rows, LANES), BF16),
+            pltpu.VMEM((count // 2, tiles, rows, LANES), BF16),
+            pltpu.VMEM((count // 4, tiles, rows, LANES), BF16),
+            pltpu.VMEM((count // 8, tiles, rows, LANES), BF16),
+            pltpu.SemaphoreType.DMA((width // group, samples, spans - 1)),
+            pltpu.SemaphoreType.DMA((width // group, samples, spans - 1)),
+            pltpu.SemaphoreType.DMA((steps, 2, count // 2)),
+            pltpu.SemaphoreType.DMA((steps, 2, count // 2)),
+        ],
+        compiler_params=pltpu.CompilerParams(
+            vmem_limit_bytes=60 << 20, collective_id=1, has_side_effects=True
+        ),
+        name="attend_back",
+    )(struct_of, query, key_value, upstream, prob)
+
+
+def pack_rows(pieces, columns):
+    return jnp.concatenate([piece.reshape(-1, columns) for piece in pieces], axis=0)
+
+
+def pack_small(pieces, columns):
+    flat = jnp.concatenate([piece.reshape(-1) for piece in pieces])
+    rows = -(-flat.shape[0] // columns)
+    rows = -(-rows // 8) * 8
+    return jnp.pad(flat, (0, rows * columns - flat.shape[0])).reshape(rows, columns)
+
+
+def unpack_rows(gathered, shapes):
+    whole, at = [], 0
+    count, _, columns = gathered.shape
+    for rows, cols in shapes:
+        held = rows * cols // columns
+        whole.append(gathered[:, at : at + held].reshape(count * rows, cols))
+        at += held
+    return whole
+
+
+def unpack_small(gathered, shapes):
+    whole, at = [], 0
+    count = gathered.shape[0]
+    flat = gathered.reshape(count, -1)
+    for shape in shapes:
+        size = 1
+        for extent in shape:
+            size *= extent
+        whole.append(flat[:, at : at + size].reshape((count * shape[0],) + shape[1:]))
+        at += size
+    return whole
+
+
+def plain_kernel(struct_ref, len_ref, q_ref, k_ref, v_ref, bias_ref, out_ref, prob_ref, acc_ref):
     sample = pl.program_id(0)
     group_at = pl.program_id(1)
     length = len_ref[struct_ref[sample]]
@@ -110,14 +586,14 @@
     out_ref[0] = acc_ref[...].astype(BF16)
 
 
-def attend(struct_of, struct_len, query, key, value, bias):
+def plain(struct_of, struct_len, query, key, value, bias):
     samples, rows, width = query.shape
     keys = key.shape[1]
     heads = bias.shape[1]
     group, windows = head_windows(width)
     each = len(windows)
     return pl.pallas_call(
-        attend_kernel,
+        plain_kernel,
         out_shape=(
             jax.ShapeDtypeStruct((samples, rows, width), BF16),
             jax.ShapeDtypeStruct((samples, heads, rows, keys), BF16),
@@ -138,11 +614,11 @@
             scratch_shapes=[pltpu.VMEM((rows, group), F32)],
         ),
         compiler_params=pltpu.CompilerParams(vmem_limit_bytes=48 << 20),
-        name="attend",
+        name="plain",
     )(struct_of, struct_len, query, key, value, bias)
 
 
-def attend_back_kernel(
+def plain_back_kernel(
     struct_ref, q_ref, k_ref, v_ref, do_ref, prob_ref, dq_ref, dk_ref, dv_ref, bias_ref,
     dq_acc, dk_acc, dv_acc, bias_acc,
 ):
@@ -184,14 +660,14 @@
         dv_ref[sample] = dv_acc[...].astype(BF16)
 
 
-def attend_back(struct_of, structs, query, key, value, upstream, prob):
+def plain_back(struct_of, structs, query, key, value, upstream, prob):
     samples, rows, width = query.shape
     keys = key.shape[1]
     heads = prob.shape[1]
     group, windows = head_windows(width)
     each = len(windows)
     return pl.pallas_call(
-        attend_back_kernel,
+        plain_back_kernel,
         out_shape=(
             jax.ShapeDtypeStruct((samples, rows, width), BF16),
             jax.ShapeDtypeStruct((samples, keys, width), BF16),
@@ -222,45 +698,11 @@
             ],
         ),
         compiler_params=pltpu.CompilerParams(vmem_limit_bytes=60 << 20),
-        name="attend_back",
+        name="plain_back",
     )(struct_of, query, key, value, upstream, prob)
 
 
-def pack_rows(pieces, columns):
-    return jnp.concatenate([piece.reshape(-1, columns) for piece in pieces], axis=0)
-
-
-def pack_small(pieces, columns):
-    flat = jnp.concatenate([piece.reshape(-1) for piece in pieces])
-    rows = -(-flat.shape[0] // columns)
-    rows = -(-rows // 8) * 8
-    return jnp.pad(flat, (0, rows * columns - flat.shape[0])).reshape(rows, columns)
-
-
-def unpack_rows(gathered, shapes):
-    whole, at = [], 0
-    count, _, columns = gathered.shape
-    for rows, cols in shapes:
-        held = rows * cols // columns
-        whole.append(gathered[:, at : at + held].reshape(count * rows, cols))
-        at += held
-    return whole
-
-
-def unpack_small(gathered, shapes):
-    whole, at = [], 0
-    count = gathered.shape[0]
-    flat = gathered.reshape(count, -1)
-    for shape in shapes:
-        size = 1
-        for extent in shape:
-            size *= extent
-        whole.append(flat[:, at : at + size].reshape((count * shape[0],) + shape[1:]))
-        at += size
-    return whole
-
-
-def per_device(
+def plain_device(
     act, cond, pair, struct_of, struct_len,
     gain_first, scale_first, scale_bias_first, shift_first,
     query_weight, query_bias, key_weight, value_weight, gate_weight, output_weight,
@@ -314,7 +756,7 @@
     key_value = jnp.stack((key_rows, value_rows)).reshape(2, samples, rows, width)
     key_value = lax.all_gather(key_value, "head", axis=2, tiled=True)
     query_split = query_rows.reshape(samples, rows, width)
-    attended, prob = attend(
+    attended, prob = plain(
         struct_of, struct_len, query_split, key_value[0], key_value[1], bias_all
     )
     attn_float = attended.reshape(total, width).astype(F32)
@@ -367,7 +809,7 @@
         outer_sum(cond_low, d_zero_second),
     )
 
-    d_query, d_key, d_value, bias_grad = attend_back(
+    d_query, d_key, d_value, bias_grad = plain_back(
         struct_of, structs, query_split, key_value[0], key_value[1],
         d_attended.reshape(samples, rows, width), prob,
     )
@@ -455,6 +897,216 @@
     )
 
 
+def per_device(
+    act, cond, pair, struct_of, struct_len,
+    gain_first, scale_first, scale_bias_first, shift_first,
+    query_weight, query_bias, key_weight, value_weight, gate_weight, output_weight,
+    pair_weight, zero_first, zero_bias_first,
+    gain_second, scale_second, scale_bias_second, shift_second,
+    swish_weight, linear_weight, down_weight, zero_second, zero_bias_second,
+    cotangent,
+):
+    samples, rows, width = act.shape
+    cond_width = cond.shape[2]
+    total = samples * rows
+    structs = pair.shape[0]
+    block = pair.shape[2]
+    count = lax.axis_size("samp")
+    small = (
+        gain_first, scale_bias_first, query_bias, zero_bias_first, gain_second,
+        scale_bias_second, zero_bias_second, pair_weight,
+    )
+    early = (scale_first, shift_first, query_weight, key_weight, value_weight, gate_weight)
+    late = (
+        output_weight, zero_first, scale_second, shift_second, swish_weight, linear_weight,
+        down_weight, zero_second,
+    )
+    small_all = lax.all_gather(pack_small(small, width), "samp", axis=0)
+    early_all = lax.all_gather(pack_rows(early, width), "samp", axis=0)
+    late_all = lax.all_gather(pack_rows(late, width), "samp", axis=0)
+    (gain_one, bias_one, bias_query, bias_zero_one, gain_two, bias_two, bias_zero_two, pair_proj_w) = (
+        unpack_small(small_all, [piece.shape for piece in small])
+    )
+    (w_scale, w_shift, w_query, w_key, w_value, w_gate) = unpack_rows(
+        early_all, [piece.shape for piece in early]
+    )
+    (w_out, w_zero, w_scale_two, w_shift_two, w_swish, w_linear, w_down, w_zero_two) = unpack_rows(
+        late_all, [piece.shape for piece in late]
+    )
+
+    pair_normed, pair_inverse = norm_rows(pair.astype(F32))
+    pair_low = pair_normed.astype(BF16)
+    pair_proj = jnp.einsum("sijc,ch->shij", pair_low, pair_proj_w, preferred_element_type=F32)
+    packed = lax.all_gather(pack_bias(pair_proj.astype(BF16)), "samp", axis=0)
+
+    act_rows = act.reshape(total, width).astype(F32)
+    cond_low = cond.reshape(total, cond_width)
+    act_normed, act_inverse = norm_rows(act_rows)
+    cond_normed, cond_inverse = norm_rows(cond_low.astype(F32))
+    cond_first = (cond_normed * gain_one.astype(F32)).astype(BF16)
+    sig_first = jax.nn.sigmoid(product(cond_first, w_scale) + bias_one.astype(F32))
+    adapted = (sig_first * act_normed + product(cond_first, w_shift)).astype(BF16)
+    key_rows = product(adapted, w_key).astype(BF16)
+    value_rows = product(adapted, w_value).astype(BF16)
+    query_rows = (product(adapted, w_query) + bias_query.astype(F32)).astype(BF16)
+    gate_sig = jax.nn.sigmoid(product(adapted, w_gate))
+    key_value = jnp.stack(
+        [key_rows_order(half.reshape(samples, rows, width), block) for half in (key_rows, value_rows)]
+    )
+    key_value = lax.all_gather(key_value, "head", axis=0)
+    query_split = query_rows.reshape(samples, rows, width)
+    attended, prob = attend(struct_of, struct_len, query_split, key_value, packed)
+    attn_float = attended.reshape(total, width).astype(F32)
+
+    gated_rows = (gate_sig * attn_float).astype(BF16)
+    branch = product(gated_rows, w_out)
+    zero_sig_first = jax.nn.sigmoid(product(cond_low, w_zero) + bias_zero_one.astype(F32))
+    middle = act_rows + zero_sig_first * branch
+    mid_normed, mid_inverse = norm_rows(middle)
+    cond_second = (cond_normed * gain_two.astype(F32)).astype(BF16)
+    sig_second = jax.nn.sigmoid(product(cond_second, w_scale_two) + bias_two.astype(F32))
+    adapted_two = (sig_second * mid_normed + product(cond_second, w_shift_two)).astype(BF16)
+    swish_pre = product(adapted_two, w_swish)
+    linear_pre = product(adapted_two, w_linear)
+    swish_sig = jax.nn.sigmoid(swish_pre)
+    hidden = (swish_pre * swish_sig * linear_pre).astype(BF16)
+    down_rows = product(hidden, w_down)
+    zero_sig_second = jax.nn.sigmoid(product(cond_low, w_zero_two) + bias_zero_two.astype(F32))
+    layer_out = (middle + zero_sig_second * down_rows).astype(BF16)
+
+    upstream = cotangent.reshape(total, width).astype(F32)
+    d_down = (upstream * zero_sig_second).astype(BF16)
+    d_zero_second = (upstream * down_rows * sigmoid_slope(zero_sig_second)).astype(BF16)
+    d_hidden = back_product(d_down, w_down)
+    d_swish = (
+        d_hidden * linear_pre * swish_sig * (1.0 + swish_pre * (1.0 - swish_sig))
+    ).astype(BF16)
+    d_linear = (d_hidden * swish_pre * swish_sig).astype(BF16)
+    d_adapted_two = back_product(d_swish, w_swish) + back_product(d_linear, w_linear)
+    d_shift_second = d_adapted_two.astype(BF16)
+    d_pre_second = (d_adapted_two * mid_normed * sigmoid_slope(sig_second)).astype(BF16)
+    d_cond_second = back_product(d_shift_second, w_shift_two) + back_product(
+        d_pre_second, w_scale_two
+    )
+    d_middle = upstream + norm_back(mid_normed, mid_inverse, d_adapted_two * sig_second)
+    d_branch = (d_middle * zero_sig_first).astype(BF16)
+    d_zero_first = (d_middle * branch * sigmoid_slope(zero_sig_first)).astype(BF16)
+    d_gated = back_product(d_branch, w_out)
+    d_gate = (d_gated * attn_float * sigmoid_slope(gate_sig)).astype(BF16)
+    d_attended = (d_gated * gate_sig).astype(BF16)
+
+    late_grads = (
+        outer_sum(gated_rows, d_branch),
+        outer_sum(cond_low, d_zero_first),
+        outer_sum(cond_second, d_pre_second),
+        outer_sum(cond_second, d_shift_second),
+        outer_sum(adapted_two, d_swish),
+        outer_sum(adapted_two, d_linear),
+        outer_sum(hidden, d_down),
+        outer_sum(cond_low, d_zero_second),
+    )
+
+    d_query, d_key_value, bias_packed = attend_back(
+        struct_of, structs, query_split, key_value, d_attended.reshape(samples, rows, width), prob, count
+    )
+    d_query = d_query.reshape(total, width)
+    d_key = key_rows_back(d_key_value[0], block).reshape(total, width)
+    d_value = key_rows_back(d_key_value[1], block).reshape(total, width)
+    bias_summed = unpack_bias(bias_packed, structs, width // HEAD_DIM)
+    pair_weight_grad = jnp.einsum("sijc,shij->ch", pair_low, bias_summed, preferred_element_type=F32)
+    pair_upstream = jnp.einsum(
+        "shij,ch->sijc", bias_summed, pair_proj_w, preferred_element_type=F32
+    )
+    pair_grad = norm_back(pair_normed, pair_inverse, pair_upstream)
+    d_adapted = (
+        back_product(d_query, w_query)
+        + back_product(d_key, w_key)
+        + back_product(d_value, w_value)
+        + back_product(d_gate, w_gate)
+    )
+    d_shift_first = d_adapted.astype(BF16)
+    d_pre_first = (d_adapted * act_normed * sigmoid_slope(sig_first)).astype(BF16)
+    d_cond_first = back_product(d_shift_first, w_shift) + back_product(d_pre_first, w_scale)
+    input_grad = d_middle + norm_back(act_normed, act_inverse, d_adapted * sig_first)
+    d_cond_normed = d_cond_first * gain_one.astype(F32) + d_cond_second * gain_two.astype(F32)
+    cond_grad = (
+        norm_back(cond_normed, cond_inverse, d_cond_normed)
+        + back_product(d_zero_first, w_zero)
+        + back_product(d_zero_second, w_zero_two)
+    )
+    early_grads = (
+        outer_sum(cond_first, d_pre_first),
+        outer_sum(cond_first, d_shift_first),
+        outer_sum(adapted, d_query),
+        outer_sum(adapted, d_key),
+        outer_sum(adapted, d_value),
+        outer_sum(adapted, d_gate),
+    )
+    small_grads = (
+        jnp.sum(d_cond_first * cond_normed, axis=0),
+        column_sum(d_pre_first),
+        column_sum(d_query),
+        column_sum(d_zero_first),
+        jnp.sum(d_cond_second * cond_normed, axis=0),
+        column_sum(d_pre_second),
+        column_sum(d_zero_second),
+        pair_weight_grad,
+    )
+
+    def pack_grads(grads, shapes):
+        pieces = [
+            grad.astype(BF16).reshape(count, shape[0] * shape[1] // width, width)
+            for grad, shape in zip(grads, shapes)
+        ]
+        return jnp.concatenate(pieces, axis=1)
+
+    def reduce(packed):
+        summed = lax.psum_scatter(packed, "samp", scatter_dimension=0, tiled=True)
+        return lax.psum(summed[0], "head").astype(F32)
+
+    late_sum = reduce(pack_grads(late_grads, [piece.shape for piece in late]))
+    early_sum = reduce(pack_grads(early_grads, [piece.shape for piece in early]))
+    small_flat = jnp.concatenate(
+        [grad.astype(BF16).reshape(count, -1) for grad in small_grads], axis=1
+    )
+    small_sum = lax.psum(
+        lax.psum_scatter(small_flat, "samp", scatter_dimension=0, tiled=True), "head"
+    ).astype(F32)
+    (g_out, g_zero, g_scale_two, g_shift_two, g_swish, g_linear, g_down, g_zero_two) = unpack_rows(
+        late_sum[None], [piece.shape for piece in late]
+    )
+    (g_scale, g_shift, g_query, g_key, g_value, g_gate) = unpack_rows(
+        early_sum[None], [piece.shape for piece in early]
+    )
+    (g_gain, g_bias, g_bias_query, g_bias_zero, g_gain_two, g_bias_two, g_bias_zero_two, g_pair) = (
+        unpack_small(small_sum, [piece.shape for piece in small])
+    )
+    return (
+        layer_out.reshape(act.shape), input_grad.reshape(act.shape), cond_grad.reshape(cond.shape),
+        pair_grad, g_gain, g_scale, g_bias, g_shift, g_query, g_bias_query, g_key, g_value, g_gate,
+        g_out, g_pair, g_zero, g_bias_zero, g_gain_two, g_scale_two, g_bias_two, g_shift_two,
+        g_swish, g_linear, g_down, g_zero_two, g_bias_zero_two,
+    )
+
+
+def fits(mesh, act, pair):
+    samples, rows, width = act.shape
+    count, spans = mesh.shape["samp"], mesh.shape["head"]
+    block = pair.shape[2]
+    tail = block - MAIN
+    heads = width // HEAD_DIM
+    return (
+        count == 8
+        and samples == 2
+        and tail > 0
+        and heads * tail == MAIN
+        and rows % block == 0
+        and rows * spans == block * count
+        and rows % 8 == 0
+        and block * count <= KEY_LANES
+    )
+
+
 def solution(mesh):
     tokens = P("samp", "head", None)
     pairs = P(None, "head", "samp", None)
@@ -464,8 +1116,12 @@
         vector, matrix, vector, matrix, matrix, vector, matrix, matrix, matrix, matrix, matrix,
         matrix, vector, vector, matrix, vector, matrix, matrix, matrix, matrix, matrix, vector,
     )
+    def choose(*arrays):
+        body = per_device if fits(mesh, arrays[0], arrays[2]) else plain_device
+        return body(*arrays)
+
     return jax.shard_map(
-        per_device,
+        choose,
         mesh=mesh,
         in_specs=(tokens, tokens, pairs, vector, P()) + weights + (tokens,),
         out_specs=(tokens, tokens, tokens, pairs) + weights,

time: 818 us -> 687 us (0.84)
  waiting for transfers between devices: 387 us -> 195 us
  Pallas kernels: 36.4 us -> 104 us
  local copies, waits for them, and re-layouts: 166 us -> 146 us
  matrix products: 91.5 us -> 105 us
    unnamed x11 -> x7, waiting for transfers between devices: 130 us -> 0.12 us
    pallas_call x1, Pallas kernels: 20.2 us -> 83 us  [attend_back(): pl.pallas_call(attend_back_kernel, out_shape=(jax.ShapeDtypeStruct((sampl...]
    reduce_scatter x2, waiting for transfers between devices: 33.5 us -> 0.01 us  [reduce(): summed = lax.psum_scatter(packed, 'samp', scatter_dimension=0, tiled=True)]
    unnamed x244 -> x246, local copies, waits for them, and re-layouts: 80.8 us -> 59.9 us
    all_gather x1 -> x0, local copies, waits for them, and re-layouts: 18.5 us -> none  [per_device(): lax.all_gather(pair_proj.astype(BF16), 'samp', axis=3, tiled=True)]
    dot_general x1, matrix products: 1.17 us -> 18.5 us  [per_device(): jnp.einsum('sijc,shij->ch', pair_low, bias_summed, preferred_element_type...]
    psum x1, waiting for transfers between devices: 82.1 us -> 65.4 us  [reduce(): return lax.psum(summed[0], 'head').astype(F32)]
    reshape x0 -> x5, local copies, waits for them, and re-layouts: none -> 15.2 us  [the longest x1 3.77 us: unpack_bias(): main = packed[:pairs].reshape(structs, heads // 2, rows, 2, MAIN)]
  transfers between devices with their start and end apart: 9 -> 7, of which waited for: 7 -> 4; matrix products, arithmetic and copies ran while one was open for 30% -> 33% of each run, Pallas kernels for 2% -> 3%
where the time goes in v1:
time: 687 us; the launch traced here: 676 us
  waiting for transfers between devices  195 us (28%)
  local copies, waits for them, and re-layouts  146 us (21%)
  matrix products  105 us (15%)
  Pallas kernels  104 us (15%)
  other arithmetic  62 us (9%)
  blocking collectives  48.7 us (7%)
  between operations  15.7 us (2%)
    pallas_call x1, Pallas kernels, attend_back(): pl.pallas_call(attend_back_kernel, out_shape=(jax.ShapeDtypeStruct((sampl...  83 us
    all_gather x1, waiting for transfers between devices, per_device(): key_value = lax.all_gather(key_value, 'head', axis=0)  68.9 us
    psum x1, waiting for transfers between devices, reduce(): return lax.psum(summed[0], 'head').astype(F32)  65.4 us
    unnamed x246, local copies, waits for them, and re-layouts  59.9 us
    all_gather x1, waiting for transfers between devices, per_device(): late_all = lax.all_gather(pack_rows(late, width), 'samp', axis=0)  40.8 us
    dot_general x1, matrix products, per_device(): jnp.einsum('shij,ch->sijc', bias_summed, pair_proj_w, preferred_element_t...  30.4 us
    convert_element_type x1, other arithmetic, per_device(): pair_low = pair_normed.astype(BF16)  28.3 us
    unnamed x1, blocking collectives  22.9 us
  transfers between devices with their start and end apart: 7, of which 4 were waited for; matrix products, arithmetic and copies ran while one was open for 33% of the time, Pallas kernels for 3%

profile of v1, /device:TPU:0, one launch (start us, length us, event | category | flops | bytes accessed | tf_op | source)
XLA Modules:
  0.0 676.5 jit_solution(6035259784796393428)
XLA Ops:
  14.4 4.8 concatenate.37
  19.2 10.9 %all_gather.29 = bf16[8,8,768]{2,1,0:T(8,128)(2,1)S(1)} all-gather(bf16[1,8,768]{2,1,0:T(8,128)(2,1)S(1)} %all_gather_reshape.3), channel_id=1, replica_groups=mesh['samp'=8,'head'=4] {'samp'}, dimensions={0}, use_global_device_ids=true | all-gather | bytes 110592 | tf_op jit(solution)/shard_map/all_gather | solution.py:924
  30.3 10.1 %convert_reduce_fusion = f32[3,136,68]{2,1,0:T(8,128)S(1)} fusion(bf16[3,136,68,128]{3,1,2,0:T(8,128)(2,1)} %param.30), kind=kLoop, calls=%fused_computation.1 | loop fusion | flops 7074720 | bytes 7213440 | tf_op jit(solution)/shard_map/reduce_sum | solution.py:22
  40.5 13.0 %fusion.8 = f32[3,136,68]{2,1,0:T(8,128)S(1)} fusion(f32[3,136,68]{2,1,0:T(8,128)S(1)} %broadcast_multiply_fusion.2, bf16[3,136,68,128]{3,1,2,0:T(8,128)(2,1)S(1)} %copy-done), kind=kLoop, calls=%fused_computation.10 | loop fusion | flops 14177184 | bytes 7324416 | tf_op jit(solution)/shard_map/reduce_sum | solution.py:23
  53.6 14.6 %fusion.13 = bf16[3,16,136,68]{3,1,2,0:T(8,128)(2,1)S(1)} fusion(bf16[128,16]{1,0:T(8,128)(2,1)S(1)} %reshape.556, f32[3,136,68]{2,1,0:T(8,128)S(1)} %add_rsqrt_fusion, f32[3,136,68]{2,1,0:T(8,128)S(1)} %broadcast_multiply_fusion.2, bf16[3,136,68,128]{3,1,2,0:T(8,128)(2,1)S(1)} %copy-done), kind=kOutput, calls=%fused_computation.32 | convolution fusion | flops 128288256 | bytes 8216320 | tf_op jit(solution)/shard_map/sijc,ch->shij/dot_general | solution.py:939
  70.5 3.3 reshape.558
  110.7 20.1 %all-gather.15.cloned.1.call-done = bf16[216,136,128]{2,1,0:T(8,128)(2,1)} async-done(((bf16[27,136,128]{2,1,0:T(8,128)(2,1)}), bf16[216,136,128]{2,1,0:T(8,128)(2,1)}) %all-gather.15.cloned.1.call-update) | async-done | bytes 7520272 | tf_op jit(solution)/shard_map/all_gather | solution.py:940
  130.8 68.9 %all-gather.13.cloned.1.call-done = bf16[8,2,136,768]{3,2,1,0:T(8,128)(2,1)} async-done(((bf16[2,2,136,768]{3,2,1,0:T(8,128)(2,1)}), bf16[8,2,136,768]{3,2,1,0:T(8,128)(2,1)}) %all-gather.13.cloned.1.call-update) | async-done | bytes 3342352 | tf_op jit(solution)/shard_map/all_gather | solution.py:956
  199.7 20.9 %attend.1 = (bf16[2,136,768]{2,1,0:T(8,128)(2,1)}, bf16[2,16,136,640]{3,2,1,0:T(8,128)(2,1)}) custom-call(s32[2]{0:T(128)} %struct_ref.3, s32[3]{0:T(128)} %len_ref.1, bf16[2,136,768]{2,1,0:T(8,128)(2,1)} %bitcast.280, bf16[4,2,2,136,768]{4,3,2,1,0:T(8,128)(2,1)} %bitcast.232, bf16[8,27,136,128]{3,2,1,0:T(8,128)(2,1)} %bitcast.249), custom_call_target="tpu_custom_call" | custom-call | tf_op jit(solution)/shard_map/attend/pallas_call | solution.py:236
  223.1 40.8 %all-gather.9.cloned.1.call-done = bf16[6912,768]{1,0:T(8,128)(2,1)} async-done(((bf16[864,768]{1,0:T(8,128)(2,1)}), bf16[6912,768]{1,0:T(8,128)(2,1)}) %all-gather.9.cloned.1.call-update) | async-done | bytes 10616848 | tf_op jit(solution)/shard_map/all_gather | solution.py:926
  268.5 6.6 fusion.91
  277.2 4.8 reshape.565
  282.0 5.3 reshape.564
  308.0 83.0 %attend_back.1 = (bf16[2,136,768]{2,1,0:T(8,128)(2,1)}, bf16[2,2,136,768]{3,2,1,0:T(8,128)(2,1)}, bf16[27,136,128]{2,1,0:T(8,128)(2,1)}) custom-call(s32[2]{0:T(128)} %struct_ref.3, bf16[2,136,768]{2,1,0:T(8,128)(2,1)} %bitcast.281, bf16[4,2,2,136,768]{4,3,2,1,0:T(8,128)(2,1)} %bitcast.233, bf16[2,136,768]{2,1,0:T(8,128)(2,1)} %bitcast.282, ...), custom_call_target="tpu_custom_call" | custom-call | tf_op jit(solution)/shard_map/attend_back/pallas_call | solution.py:494
  416.8 5.0 reshape.603
  424.6 5.0 reshape.602
  452.4 3.8 reshape.574
  461.5 30.4 %fusion.78 = (f32[3,136,68]{2,1,0:T(8,128)S(1)}, f32[3,136,68]{2,1,0:T(8,128)S(1)}, f32[3,136,68,128]{3,2,1,0:T(8,128)S(1)}) fusion(f32[3,136,68]{2,1,0:T(8,128)S(1)} %copy-done.55, f32[3,136,68]{2,1,0:T(8,128)S(1)} %copy-done.44, bf16[3,136,68,128]{3,1,2,0:T(8,128)(2,1)} %param.30, bf16[128,16]{1,0:T(8,128)(2,1)} %copy-done.72, ...), kind=kOutput, calls=%fused_computation.222 | convolution fusion | flops 136666944 | bytes 22643200 | tf_op jit(solution)/shard_map/shij,ch->sijc/dot_general | solution.py:1017
  491.9 28.3 %fusion.4 = (bf16[3,136,68,128]{3,2,1,0:T(8,128)(2,1)S(1)}, f32[3,136,68,128]{3,2,1,0:T(8,128)}) fusion(f32[3,136,68]{2,1,0:T(8,128)S(1)} %copy-done.55, f32[3,136,68]{2,1,0:T(8,128)S(1)} %copy-done.44, bf16[3,136,68,128]{3,1,2,0:T(8,128)(2,1)S(1)} %bitcast.228, f32[3,136,68]{2,1,0:T(8,128)S(1)} %broadcast_multiply_fusion, ...), kind=kLoop, calls=%fused_computation.6 | loop fusion | flops 28409856 | bytes 43058688 | tf_op jit(solution)/shard_map/convert_element_type | solution.py:938
  520.3 18.5 %fusion.43 = bf16[128,16]{0,1:T(8,128)(2,1)S(1)} fusion(bf16[3,136,68,128]{3,2,1,0:T(8,128)(2,1)S(1)} %get-tuple-element.175, bf16[3,16,136,4]{3,1,2,0:T(8,128)(2,1)S(1)} %bitcast.292, bf16[3,16,136,64]{3,1,2,0:T(8,128)(2,1)S(1)} %bitcast.290), kind=kOutput, calls=%fused_computation.90 | convolution fusion | flops 115417088 | bytes 7994368 | tf_op jit(solution)/shard_map/sijc,shij->ch/dot_general | solution.py:1016
  539.3 22.9 %all-reduce.2 = bf16[8,832]{1,0:T(8,128)(2,1)S(1)} all-reduce(bf16[8,832]{1,0:T(8,128)(2,1)S(1)} %concatenate.45), channel_id=6, replica_groups=mesh['samp'=8,'head'=4] {'samp'}, use_global_device_ids=true, to_apply=%region_23.24.clone | all-reduce | flops 6656 | bytes 26624
  562.8 14.9 %psum.21 = bf16[1,832]{1,0:T(2,128)(2,1)S(1)} all-reduce(bf16[1,832]{1,0:T(2,128)(2,1)S(1)} %constant_dynamic-slice_fusion), channel_id=1, replica_groups=mesh['samp'=8,'head'=4] {'head'}, use_global_device_ids=true, to_apply=%region_24.25 | all-reduce | flops 832 | bytes 3328 | tf_op jit(solution)/shard_map/psum | solution.py:1072
  579.2 13.5 %copy.98 = f32[3,136,68,128]{3,1,2,0:T(8,128)} copy(f32[3,136,68,128]{3,2,1,0:T(8,128)} %get-tuple-element.176) | data formatting | bytes 28409856
  596.3 65.4 %all-reduce.6.cloned.1.call-done = (bf16[1,480,768]{2,1,0:T(8,128)(2,1)}, bf16[1,864,768]{2,1,0:T(8,128)(2,1)}) async-done(((bf16[1,480,768]{2,1,0:T(8,128)(2,1)}, bf16[1,864,768]{2,1,0:T(8,128)(2,1)}), (bf16[1,480,768]{2,1,0:T(8,128)(2,1)}, bf16[1,864,768]{2,1,0:T(8,128)(2,1)})) %all-reduce.6.cloned.1.call-update) | async-done | bytes 2064400 | tf_op jit(solution)/shard_map/psum | solution.py:1065
  (406 shorter events, 145.9 us)
Async XLA Ops:
  7.2 75.7 %all-gather.11.cloned.1.call-start = ((), (), s32[]{:S(2)}) async-start(), calls=%async_computation.5 | async-start | bytes 6635520 | tf_op jit(solution)/shard_map/all_gather | solution.py:925
  13.6 117.1 %all-gather.15.cloned.1.call-start = ((), (), s32[]{:S(2)}) async-start(), calls=%async_computation.7 | async-start | bytes 8460288 | tf_op jit(solution)/shard_map/all_gather | solution.py:940
  30.3 23.3 %copy-start.72 = (bf16[128,16]{1,0:T(8,128)(2,1)}, bf16[128,16]{1,0:T(8,128)(2,1)S(1)}, u32[]{:S(2)}) copy-start(bf16[128,16]{1,0:T(8,128)(2,1)S(1)} %reshape.556) | copy-start | bytes 12292
  79.6 120.1 %all-gather.13.cloned.1.call-start = ((), (), s32[]{:S(2)}) async-start(), calls=%async_computation.6 | async-start | bytes 4177920 | tf_op jit(solution)/shard_map/all_gather | solution.py:956
  88.1 132.5 %copy-start.24 = (bf16[272,768]{1,0:T(8,128)(2,1)}, bf16[272,768]{1,0:T(8,128)(2,1)S(1)}, u32[]{:S(2)}) copy-start(bf16[272,768]{1,0:T(8,128)(2,1)S(1)} %fusion.36) | copy-start | bytes 1253380
  89.5 19.9 %copy-start.20 = (bf16[8,96,768]{2,1,0:T(8,128)(2,1)}, bf16[8,96,768]{2,1,0:T(8,128)(2,1)S(1)}, u32[]{:S(2)}) copy-start(bf16[8,96,768]{2,1,0:T(8,128)(2,1)S(1)} %get-tuple-element.179) | copy-start | bytes 3538948
  91.8 172.1 %all-gather.9.cloned.1.call-start = ((), (), s32[]{:S(2)}) async-start(), calls=%async_computation.4 | async-start | bytes 11943936 | tf_op jit(solution)/shard_map/all_gather | solution.py:926
  106.4 471.9 %reduce-scatter.3.cloned.1.call-start = ((), (), s32[]{:S(2)}) async-start(), calls=%async_computation.2 | async-start | bytes 6635520 | tf_op jit(solution)/shard_map/reduce_scatter | solution.py:1064
  199.7 20.9 %copy-start.22 = (bf16[8,96,768]{2,1,0:T(8,128)(2,1)S(1)}, bf16[8,96,768]{2,1,0:T(8,128)(2,1)}, u32[]{:S(2)}) copy-start(bf16[8,96,768]{2,1,0:T(8,128)(2,1)} %get-tuple-element.180) | copy-start | bytes 3538948
  223.0 52.0 %copy-start.60 = (bf16[272,768]{1,0:T(8,128)(2,1)}, bf16[272,768]{1,0:T(8,128)(2,1)S(1)}, u32[]{:S(2)}) copy-start(bf16[272,768]{1,0:T(8,128)(2,1)S(1)} %get-tuple-element.242) | copy-start | bytes 1253380
  268.5 20.4 %copy-start.15 = (bf16[8,48,768]{2,1,0:T(8,128)(2,1)}, bf16[8,48,768]{2,1,0:T(8,128)(2,1)S(1)}, u32[]{:S(2)}) copy-start(bf16[8,48,768]{2,1,0:T(8,128)(2,1)S(1)} %get-tuple-element.172) | copy-start | bytes 1769476
  304.4 95.1 %copy-start.27 = (bf16[272,768]{1,0:T(8,128)(2,1)}, bf16[272,768]{1,0:T(8,128)(2,1)S(1)}, u32[]{:S(2)}) copy-start(bf16[272,768]{1,0:T(8,128)(2,1)S(1)} %get-tuple-element.157) | copy-start | bytes 1253380
  412.7 165.6 %reduce-scatter.5.cloned.1.call-start = ((), (), s32[]{:S(2)}) async-start(), calls=%async_computation.3 | async-start | bytes 11943936 | tf_op jit(solution)/shard_map/reduce_scatter | solution.py:1064
  444.8 216.9 %all-reduce.6.cloned.1.call-start = ((), (), s32[]{:S(2)}) async-start(), calls=%async_computation.8 | async-start | bytes 4128768 | tf_op jit(solution)/shard_map/psum | solution.py:1065
  461.4 30.5 %slice-start = ((s8[7102464]{0:T(1024)(128)(4,1)}), s8[4194304]{0:T(1024)(128)(4,1)S(1)}, s32[]{:S(2)}) async-start(s8[7102464]{0:T(1024)(128)(4,1)} %bitcast.227), calls=%async_computation.9 | async-start | bytes 8388608
  461.4 30.4 %slice-start.1 = ((s8[7102464]{0:T(1024)(128)(4,1)}), s8[2908160]{0:T(1024)(128)(4,1)S(1)}, s32[]{:S(2)}) async-start(s8[7102464]{0:T(1024)(128)(4,1)} %bitcast.227), calls=%async_computation.10 | async-start | bytes 5816320
  491.9 28.3 %copy-start.49 = (bf16[3,8,2,136,64]{4,2,1,3,0:T(2,128)(2,1)S(1)}, bf16[3,8,2,136,64]{4,2,1,3,0:T(2,128)(2,1)}, u32[]{:S(2)}) copy-start(bf16[3,8,2,136,64]{4,2,1,3,0:T(2,128)(2,1)} %copy.91) | copy-start | bytes 2506756
  520.3 18.8 %copy-start.88 = (bf16[8,96]{1,0:T(8,128)(2,1)S(1)}, bf16[8,96]{1,0:T(8,128)(2,1)}, u32[]{:S(2)}) copy-start(bf16[8,96]{1,0:T(8,128)(2,1)} %reshape.580) | copy-start | bytes 4612
  520.3 18.8 %copy-start.89 = (bf16[8,96]{1,0:T(8,128)(2,1)S(1)}, bf16[8,96]{1,0:T(8,128)(2,1)}, u32[]{:S(2)}) copy-start(bf16[8,96]{1,0:T(8,128)(2,1)} %reshape.579) | copy-start | bytes 4612
  520.3 18.8 %copy-start.90 = (bf16[8,96]{1,0:T(8,128)(2,1)S(1)}, bf16[8,96]{1,0:T(8,128)(2,1)}, u32[]{:S(2)}) copy-start(bf16[8,96]{1,0:T(8,128)(2,1)} %reshape.581) | copy-start | bytes 4612
  520.3 18.8 %copy-start.91 = (bf16[8,96]{1,0:T(8,128)(2,1)S(1)}, bf16[8,96]{1,0:T(8,128)(2,1)}, u32[]{:S(2)}) copy-start(bf16[8,96]{1,0:T(8,128)(2,1)} %reshape.578) | copy-start | bytes 4612
  520.3 18.8 %copy-start.92 = (bf16[8,96]{1,0:T(8,128)(2,1)S(1)}, bf16[8,96]{1,0:T(8,128)(2,1)}, u32[]{:S(2)}) copy-start(bf16[8,96]{1,0:T(8,128)(2,1)} %reshape.577) | copy-start | bytes 4612
  520.3 18.8 %copy-start.93 = (bf16[8,48]{1,0:T(8,128)(2,1)S(1)}, bf16[8,48]{1,0:T(8,128)(2,1)}, u32[]{:S(2)}) copy-start(bf16[8,48]{1,0:T(8,128)(2,1)} %convert_element_type.331) | copy-start | bytes 2308
  520.3 18.8 %copy-start.94 = (bf16[8,48]{1,0:T(8,128)(2,1)S(1)}, bf16[8,48]{1,0:T(8,128)(2,1)}, u32[]{:S(2)}) copy-start(bf16[8,48]{1,0:T(8,128)(2,1)} %convert_element_type.333) | copy-start | bytes 2308
  (92 other events, 417.2 us)
Sparse Core Ops, SparseCore 0:
  13.7 46.7 all-gather.10
  79.7 51.0 all-gather.14
  132.9 66.7 all-gather.12
  201.4 62.4 all-gather.8
  412.9 62.4 reduce-scatter.2
  479.3 82.5 reduce-scatter.4
  578.5 83.1 all-reduce.5

commit v2 on v1

--- a/solution.py
+++ b/solution.py
@@ -104,21 +104,12 @@
     return jnp.concatenate(parts, axis=1)
 
 
-def pack_bias(bias):
-    structs, heads, rows, block = bias.shape
-    main = bias[..., :MAIN].reshape(structs, heads // 2, 2, rows, MAIN)
-    main = main.transpose(0, 1, 3, 2, 4).reshape(-1, rows, LANES)
-    tail = bias[..., MAIN:].transpose(0, 2, 1, 3).reshape(structs, rows, -1)
-    tail = jnp.pad(tail, ((0, 0), (0, 0), (0, LANES - tail.shape[2])))
-    return jnp.concatenate((main, tail), axis=0)
-
-
 def unpack_bias(packed, structs, heads):
     rows = packed.shape[1]
     pairs = structs * heads // 2
     main = packed[:pairs].reshape(structs, heads // 2, rows, 2, MAIN)
     main = main.transpose(0, 1, 3, 2, 4).reshape(structs, heads, rows, MAIN)
-    tail = packed[pairs:, :, :MAIN].reshape(structs, rows, heads, -1).transpose(0, 2, 1, 3)
+    tail = packed[pairs:, :, :MAIN].reshape(structs, rows, -1, heads).transpose(0, 3, 1, 2)
     return jnp.concatenate((main, tail), axis=3)
 
 
@@ -127,8 +118,8 @@
     source = lax.broadcasted_iota(jnp.int32, (lanes, lanes), 0)
     target = lax.broadcasted_iota(jnp.int32, (lanes, lanes), 1)
     owner = source // (heads * tail)
-    head = source // tail % heads
-    spot = head * (count * tail) + owner * tail + source % tail
+    head = source % heads
+    spot = head * (count * tail) + owner * tail + source // heads % tail
     return jnp.where(spot == target, 1.0, 0.0).astype(BF16)
 
 
@@ -150,38 +141,332 @@
     return jnp.where(spare < 0, main_at, past)
 
 
-def attend_kernel(
-    struct_ref, len_ref, q_ref, kv_ref, pack_ref, out_ref, prob_ref, key_ref, value_ref, tail_ref, acc_ref
+def flip(index, bit):
+    return index + bit - 2 * bit * lax.rem(lax.div(index, bit), 2)
+
+
+def flips(index, bits):
+    spots = [index]
+    for bit in bits:
+        spots = spots + [flip(spot, bit) for spot in spots]
+    return spots
+
+
+def reduce_orders(count):
+    bits = []
+    bit = 2
+    while bit < count:
+        bits.append(bit)
+        bit *= 2
+    half = len(bits) // 2
+    return ([1] + bits, [1] + bits[half:] + bits[:half])
+
+
+def greet(partners):
+    barrier = pltpu.get_barrier_semaphore()
+    for partner in partners:
+        pl.semaphore_signal(barrier, inc=1, device_id=partner, device_id_type=MESH)
+    pl.semaphore_wait(barrier, len(partners))
+
+
+def send(source, target, send_sem, recv_sem, device):
+    return pltpu.make_async_remote_copy(
+        src_ref=source, dst_ref=target, send_sem=send_sem, recv_sem=recv_sem,
+        device_id=device, device_id_type=MESH,
+    )
+
+
+def sigmoid(values):
+    return 1.0 / (1.0 + jnp.exp(-values))
+
+
+def one_hot(shape, source_of):
+    target = lax.broadcasted_iota(jnp.int32, shape, 0)
+    source = lax.broadcasted_iota(jnp.int32, shape, 1)
+    return jnp.where(source == source_of(target), 1.0, 0.0).astype(BF16)
+
+
+def key_row_of(place, block, pieces):
+    tail = block - MAIN
+    main_at = place // MAIN * block + place % MAIN
+    spare = place - pieces * MAIN
+    tail_at = spare // tail * block + MAIN + spare % tail
+    return jnp.where(place < pieces * MAIN, main_at, tail_at)
+
+
+def front_kernel(
+    struct_ref, len_ref, act_ref, cond_ref, small_ref, pair_ref,
+    scale_in, shift_in, key_in, value_in, query_in, gate_in,
+    out_ref, prob_ref, adapted_ref, sig_ref, gate_ref, query_ref, kv_ref, full_ref,
+    scale_w, shift_w, key_w, value_w, query_w, gate_w,
+    small_all, pack_ref, pair_buf, tails_ref, keys_ref, values_ref, tail_ref, acc_ref,
+    pair_sem, own_sem, small_send, small_recv, gather_send, gather_recv, pack_send, pack_recv,
+    span_send, span_recv,
 ):
-    samples, rows, width = q_ref.shape
+    total, width = act_ref.shape
+    samples, rows = prob_ref.shape[0], prob_ref.shape[2]
     count = pack_ref.shape[0]
     spans = kv_ref.shape[0]
     heads = width // HEAD_DIM
-    block = rows * spans // count
+    structs = pair_ref.shape[0]
+    block = pair_ref.shape[2]
     tail = block - MAIN
-    structs = pack_ref.shape[1] // (heads // 2 + 1)
-    main_rows = rows // block * MAIN
+    pieces = rows // block
+    main_rows = pieces * MAIN
     keys = count * block
+    pairs = heads // 2
     group, windows = head_windows(width)
+    me = lax.axis_index("samp")
+    my_span = lax.axis_index("head")
+    reduce_pair = reduce_orders(count)
+    orders = [order[1:] + order[:1] for order in reduce_pair]
+    bits = sorted(reduce_pair[0])
+    steps = len(bits)
+    peers = flips(me, bits)
+
+    shards = (scale_in, shift_in, key_in, value_in, query_in, gate_in)
+    wholes = (scale_w, shift_w, key_w, value_w, query_w, gate_w)
+    owns = [
+        pltpu.make_async_copy(shard, whole.at[me], own_sem.at[at])
+        for at, (shard, whole) in enumerate(zip(shards, wholes))
+    ]
+    for copy in owns:
+        copy.start()
+
+    def pair_copy(place):
+        slot = lax.rem(place, 2)
+        struct = lax.div(place, rows // 8)
+        first = pl.multiple_of(lax.rem(place, rows // 8) * 8, 8)
+        return pltpu.make_async_copy(
+            pair_ref.at[struct, pl.ds(first, 8)], pair_buf.at[slot], pair_sem.at[slot]
+        )
+
+    pair_copy(0).start()
+    small_all[me] = small_ref[...]
+    greet(
+        [dict(samp=peer) for peer in peers[1:]]
+        + [dict(head=lax.rem(my_span + away, spans)) for away in range(1, spans)]
+    )
+    for at in range(1, count):
+        send(
+            small_ref, small_all.at[me], small_send.at[at], small_recv.at[at], dict(samp=peers[at])
+        ).start()
+
+    def gather_copies(which, step, sending):
+        order = orders[which % 2]
+        held = flips(me, order[:step])
+        copies = []
+        for at, spot in enumerate(held):
+            slot = spot if sending else flip(spot, order[step])
+            copies.append(
+                send(
+                    wholes[which].at[slot], wholes[which].at[slot],
+                    gather_send.at[which, step, at], gather_recv.at[which, step, at],
+                    dict(samp=flip(me, order[step])),
+                )
+            )
+        return copies
+
+    def gather_start(pair_at, step):
+        for which in (2 * pair_at, 2 * pair_at + 1):
+            for copy in gather_copies(which, step, True):
+                copy.start()
+
+    def gather_wait(pair_at, step):
+        for which in (2 * pair_at, 2 * pair_at + 1):
+            for copy in gather_copies(which, step, False):
+                copy.wait_recv()
+
+    tiles = pack_ref.shape[1]
+    halves = (pl.ds(0, tiles // 2), pl.ds(tiles // 2, tiles - tiles // 2))
+
+    def pack_copies(half, step, sending):
+        order = orders[half]
+        copies = []
+        for at, spot in enumerate(flips(me, order[:step])):
+            slot = spot if sending else flip(spot, order[step])
+            copies.append(
+                send(
+                    pack_ref.at[slot, halves[half]], pack_ref.at[slot, halves[half]],
+                    pack_send.at[half, step, at], pack_recv.at[half, step, at],
+                    dict(samp=flip(me, order[step])),
+                )
+            )
+        return copies
+
+    def pack_start(step):
+        for half in range(2):
+            for copy in pack_copies(half, step, True):
+                copy.start()
+
+    def pack_wait(step):
+        for half in range(2):
+            for copy in pack_copies(half, step, False):
+                copy.wait_recv()
+
+    for copy in owns:
+        copy.wait()
+    gather_start(0, 0)
+    gather_start(1, 0)
+
+    for at in range(1, count):
+        send(
+            small_ref, small_all.at[peers[at]], small_send.at[at], small_recv.at[at], dict(samp=peers[at])
+        ).wait_recv()
+    full = small_all[0].astype(F32)
+    for at in range(1, count):
+        full = full + small_all[at].astype(F32)
+    full_ref[...] = full
+    project = full[8:, :LANES].astype(BF16)
+    swap_rows = one_hot((8 * pairs, 8 * pairs), lambda row: row % 8 * pairs + row // 8)
+
+    def pair_block(place, carry):
+        slot = lax.rem(place, 2)
+        struct = lax.div(place, rows // 8)
+        first = pl.multiple_of(lax.rem(place, rows // 8) * 8, 8)
+
+        @pl.when(place + 1 < structs * (rows // 8))
+        def _():
+            pair_copy(place + 1).start()
+
+        pair_copy(place).wait()
+        values = pair_buf[slot].astype(F32)
+        centered = values - jnp.mean(values, axis=2, keepdims=True)
+        variance = jnp.mean(centered * centered, axis=2, keepdims=True)
+        normed = centered * lax.rsqrt(variance + EPSILON)
+        low = normed.astype(BF16)
+        rows_of = []
+        for at in range(8):
+            both = dot_nt(project, low[at, :MAIN])
+            wide = jnp.concatenate((both[:pairs], both[pairs:]), axis=1)
+            rows_of.append(wide)
+        mixed = dot_nn(swap_rows, jnp.concatenate(rows_of, axis=0).astype(BF16))
+        for at in range(pairs):
+            pack_ref[me, struct * pairs + at, pl.ds(first, 8)] = mixed[at * 8 : (at + 1) * 8].astype(BF16)
+        for at in range(tail):
+            tails_ref[struct, at, pl.ds(first, 8)] = normed[:, MAIN + at]
+        return carry
+
+    blocks = structs * (rows // 8)
+    cuts = [blocks * at // 8 for at in range(9)]
+    lax.fori_loop(cuts[0], cuts[1], pair_block, 0)
+    gather_wait(0, 0)
+    gather_start(0, 1)
+    lax.fori_loop(cuts[1], cuts[3], pair_block, 0)
+    gather_wait(1, 0)
+    gather_start(1, 1)
+    gather_start(2, 0)
+    lax.fori_loop(cuts[3], cuts[5], pair_block, 0)
+    gather_wait(0, 1)
+    gather_start(0, 2)
+    lax.fori_loop(cuts[5], cuts[7], pair_block, 0)
+    gather_wait(1, 1)
+    gather_start(1, 2)
+    lax.fori_loop(cuts[7], cuts[8], pair_block, 0)
+    gather_wait(2, 0)
+    gather_start(2, 1)
+
+    lane = lax.broadcasted_iota(jnp.int32, (heads, heads), 0)
+    other = lax.broadcasted_iota(jnp.int32, (heads, heads), 1)
+    natural = jnp.where(other == lane // 2 + lane % 2 * pairs, 1.0, 0.0).astype(BF16)
+    in_order = dot_nn(natural, project).astype(BF16)
+    for struct in range(structs):
+        parts = []
+        for at in range(tail):
+            parts.append(dot_nt(tails_ref[struct, at].astype(BF16), in_order))
+        parts.append(jnp.zeros((rows, LANES - tail * heads), F32))
+        pack_ref[me, structs * pairs + struct] = jnp.concatenate(parts, axis=1).astype(BF16)
+    pack_start(0)
+
+    gain_one = full[0:1, : cond_ref.shape[1]]
+    act_normed, _ = norm_rows(act_ref[...].astype(F32))
+    cond_normed, _ = norm_rows(cond_ref[...].astype(F32))
+    cond_first = (cond_normed * gain_one).astype(BF16)
+    gather_wait(0, 2)
+    scale = scale_w[...].reshape(-1, width)
+    shift = shift_w[...].reshape(-1, width)
+    sig_first = sigmoid(dot_nn(cond_first, scale) + full[1:2])
+    adapted = sig_first * act_normed + dot_nn(cond_first, shift)
+    sig_ref[...] = sig_first
+    adapted_ref[...] = adapted.astype(BF16)
+    reorder = one_hot((rows, rows), lambda row: key_row_of(row, block, pieces))
+    gather_wait(1, 2)
+    for which, whole in ((0, key_w), (1, value_w)):
+        for sample in range(samples):
+            ordered = dot_nn(
+                reorder, adapted[sample * rows : (sample + 1) * rows].astype(BF16)
+            ).astype(BF16)
+            kv_ref[my_span, which, sample] = dot_nn(ordered, whole[...].reshape(-1, width)).astype(BF16)
+
+    def span_move(way, step, which, sending):
+        delta = 1 - 2 * way
+        shard = my_span - delta * step if sending else my_span - delta * (step + 1)
+        target = my_span + delta
+        there = (shard >= 0) & (shard < spans)
+        if sending:
+            there = there & (target >= 0) & (target < spans)
+        copy = send(
+            kv_ref.at[shard, which], kv_ref.at[shard, which],
+            span_send.at[way, step, which], span_recv.at[way, step, which],
+            dict(head=target if sending else my_span - delta),
+        )
+        return there, copy
+
+    def span_start(step, which):
+        for way in range(2):
+            there, copy = span_move(way, step, which, True)
+            pl.when(there)(copy.start)
+
+    def span_wait(step, which):
+        for way in range(2):
+            there, copy = span_move(way, step, which, False)
+            pl.when(there)(copy.wait_recv)
+
+    span_start(0, 0)
+    span_start(0, 1)
+    gather_wait(2, 1)
+    gather_start(2, 2)
+    pack_wait(0)
+    pack_start(1)
+    gather_wait(2, 2)
+    low = adapted.astype(BF16)
+    query = dot_nn(low, query_w[...].reshape(-1, width)) + full[2:3]
+    for sample in range(samples):
+        query_ref[sample] = query[sample * rows : (sample + 1) * rows].astype(BF16)
+    span_wait(0, 0)
+    span_start(1, 0)
+    gate_ref[...] = sigmoid(dot_nn(low, gate_w[...].reshape(-1, width)))
+    span_wait(0, 1)
+    span_start(1, 1)
+    for step in range(1, spans - 1):
+        for which in range(2):
+            if step == 1 and which == 1:
+                pack_wait(1)
+                pack_start(2)
+            span_wait(step, which)
+            if step + 1 < spans - 1:
+                span_start(step + 1, which)
+    pack_wait(2)
+
     switch = tail_switch(count, heads, tail)
     places = key_places(count, block)
-    key_ref[keys:] = jnp.zeros_like(key_ref[keys:])
-    value_ref[keys:] = jnp.zeros_like(value_ref[keys:])
+    keys_ref[keys:] = jnp.zeros_like(keys_ref[keys:])
+    values_ref[keys:] = jnp.zeros_like(values_ref[keys:])
 
     def one_sample(sample, carry):
         struct = struct_ref[sample]
         valid = places < len_ref[struct]
         for span in range(spans):
-            for which, held in ((0, key_ref), (1, value_ref)):
+            for which, held in ((0, keys_ref), (1, values_ref)):
                 held[span * main_rows : (span + 1) * main_rows] = kv_ref[span, which, sample, :main_rows]
                 spot = count * MAIN + span * (rows - main_rows)
                 held[spot : spot + rows - main_rows] = kv_ref[span, which, sample, main_rows:]
-        tiles = []
+        tiles_of = []
         for pair in range(count // 2):
-            even = pack_ref[2 * pair, structs * heads // 2 + struct]
-            odd = swap_halves(pack_ref[2 * pair + 1, structs * heads // 2 + struct])
-            tiles.append(jnp.where(low_half(even), even, odd))
-        mixed = dot_nn(jnp.concatenate(tiles, axis=1), switch).astype(BF16)
+            even = pack_ref[2 * pair, structs * pairs + struct]
+            odd = swap_halves(pack_ref[2 * pair + 1, structs * pairs + struct])
+            tiles_of.append(jnp.where(low_half(even), even, odd))
+        mixed = dot_nn(jnp.concatenate(tiles_of, axis=1), switch).astype(BF16)
         for at in range(count // 2):
             tail_ref[at] = mixed[:, at * LANES : (at + 1) * LANES]
 
@@ -190,7 +475,7 @@
             for at, (start, span, offset) in enumerate(windows):
                 lanes = pl.ds(pl.multiple_of(place * group + start, LANES), span)
                 mask = head_mask(span, offset)
-                tile = struct * (heads // 2) + place * (len(windows) // 2) + at // 2
+                tile = struct * pairs + place * (len(windows) // 2) + at // 2
                 bias = []
                 for pair in range(count // 2):
                     even = pack_ref[2 * pair, tile]
@@ -203,9 +488,9 @@
                 rest = tail_ref[place * (len(windows) // per_tile) + at // per_tile]
                 turn = at % per_tile * count * tail
                 bias.append(pltpu.roll(rest, LANES - turn, 1) if turn else rest)
-                query = q_ref[sample, :, lanes]
+                query = query_ref[sample, :, lanes]
                 query = jnp.where(mask, query, jnp.zeros_like(query))
-                scores = dot_nt(query, key_ref[:, lanes]) * HEAD_DIM ** (-0.5) + jnp.concatenate(
+                scores = dot_nt(query, keys_ref[:, lanes]) * HEAD_DIM ** (-0.5) + jnp.concatenate(
                     bias, axis=1
                 ).astype(F32)
                 scores = jnp.where(valid, scores, NEG_BIG)
@@ -213,7 +498,7 @@
                 weights = weights * (1.0 / jnp.sum(weights, axis=1, keepdims=True))
                 weights = weights.astype(BF16)
                 prob_ref[sample, place * len(windows) + at] = weights
-                mixed = dot_nn(weights, value_ref[:, lanes])
+                mixed = dot_nn(weights, values_ref[:, lanes])
                 within = slice(start, start + span)
                 acc_ref[:, within] += jnp.where(mask, mixed, 0.0)
             out_ref[sample, :, pl.ds(pl.multiple_of(place * group, LANES), group)] = acc_ref[
@@ -225,66 +510,78 @@
 
     lax.fori_loop(0, samples, one_sample, 0)
 
-
-def attend(struct_of, struct_len, query, key_value, packed):
-    samples, rows, width = query.shape
+    for at in range(1, count):
+        send(
+            small_ref, small_all.at[me], small_send.at[at], small_recv.at[at], dict(samp=peers[at])
+        ).wait_send()
+    for which in range(len(wholes)):
+        for step in range(steps):
+            for copy in gather_copies(which, step, True):
+                copy.wait_send()
+    for half in range(2):
+        for step in range(steps):
+            for copy in pack_copies(half, step, True):
+                copy.wait_send()
+    for step in range(spans - 1):
+        for which in range(2):
+            for way in range(2):
+                there, copy = span_move(way, step, which, True)
+                pl.when(there)(copy.wait_send)
+
+
+def front(struct_of, struct_len, act, cond, small, pair, shards, samples, count, spans):
+    total, width = act.shape
+    rows = total // samples
+    structs, block = pair.shape[0], pair.shape[2]
+    heads = width // HEAD_DIM
     group, windows = head_windows(width)
-    count = packed.shape[0]
-    heads = width // HEAD_DIM
+    tail = block - MAIN
+    tiles = structs * (heads // 2 + 1)
+    steps = count.bit_length() - 1
     vmem = pl.BlockSpec(memory_space=pltpu.VMEM)
     smem = pl.BlockSpec(memory_space=pltpu.SMEM)
+    far = pl.BlockSpec(memory_space=pl.ANY)
+    dma = pltpu.SemaphoreType.DMA
     return pl.pallas_call(
-        attend_kernel,
+        front_kernel,
         out_shape=(
             jax.ShapeDtypeStruct((samples, rows, width), BF16),
             jax.ShapeDtypeStruct((samples, heads, rows, KEY_LANES), BF16),
-        ),
-        in_specs=[smem, smem, vmem, vmem, vmem],
-        out_specs=[vmem, vmem],
+            jax.ShapeDtypeStruct((total, width), BF16),
+            jax.ShapeDtypeStruct((total, width), F32),
+            jax.ShapeDtypeStruct((total, width), F32),
+            jax.ShapeDtypeStruct((samples, rows, width), BF16),
+            jax.ShapeDtypeStruct((spans, 2, samples, rows, width), BF16),
+            jax.ShapeDtypeStruct(small.shape, F32),
+        )
+        + tuple(jax.ShapeDtypeStruct((count,) + shard.shape, BF16) for shard in shards),
+        in_specs=[smem, smem, vmem, vmem, vmem] + [far] * 7,
+        out_specs=[vmem] * 14,
         scratch_shapes=[
+            pltpu.VMEM((count,) + small.shape, BF16),
+            pltpu.VMEM((count, tiles, rows, LANES), BF16),
+            pltpu.VMEM((2, 8, block, LANES), BF16),
+            pltpu.VMEM((structs, tail, rows, LANES), F32),
             pltpu.VMEM((KEY_LANES, width), BF16),
             pltpu.VMEM((KEY_LANES, width), BF16),
             pltpu.VMEM((count // 2, rows, LANES), BF16),
             pltpu.VMEM((rows, group), F32),
+            dma((2,)),
+            dma((len(shards),)),
+            dma((count,)),
+            dma((count,)),
+            dma((len(shards), steps, count // 2)),
+            dma((len(shards), steps, count // 2)),
+            dma((2, steps, count // 2)),
+            dma((2, steps, count // 2)),
+            dma((2, spans - 1, 2)),
+            dma((2, spans - 1, 2)),
         ],
-        compiler_params=pltpu.CompilerParams(vmem_limit_bytes=56 << 20),
-        name="attend",
-    )(struct_of, struct_len, query, key_value, packed)
-
-
-def flip(index, bit):
-    return index + bit - 2 * bit * lax.rem(lax.div(index, bit), 2)
-
-
-def flips(index, bits):
-    spots = [index]
-    for bit in bits:
-        spots = spots + [flip(spot, bit) for spot in spots]
-    return spots
-
-
-def reduce_orders(count):
-    bits = []
-    bit = 2
-    while bit < count:
-        bits.append(bit)
-        bit *= 2
-    half = len(bits) // 2
-    return ([1] + bits, [1] + bits[half:] + bits[:half])
-
-
-def greet(partners):
-    barrier = pltpu.get_barrier_semaphore()
-    for partner in partners:
-        pl.semaphore_signal(barrier, inc=1, device_id=partner, device_id_type=MESH)
-    pl.semaphore_wait(barrier, len(partners))
-
-
-def send(source, target, send_sem, recv_sem, device):
-    return pltpu.make_async_remote_copy(
-        src_ref=source, dst_ref=target, send_sem=send_sem, recv_sem=recv_sem,
-        device_id=device, device_id_type=MESH,
-    )
+        compiler_params=pltpu.CompilerParams(
+            vmem_limit_bytes=60 << 20, collective_id=2, has_side_effects=True
+        ),
+        name="front",
+    )(struct_of, struct_len, act, cond, small, pair, *shards)
 
 
 def attend_back_kernel(
@@ -914,48 +1211,49 @@
     count = lax.axis_size("samp")
     small = (
         gain_first, scale_bias_first, query_bias, zero_bias_first, gain_second,
-        scale_bias_second, zero_bias_second, pair_weight,
-    )
-    early = (scale_first, shift_first, query_weight, key_weight, value_weight, gate_weight)
+        scale_bias_second, zero_bias_second,
+    )
+    early = (scale_first, shift_first, key_weight, value_weight, query_weight, gate_weight)
     late = (
         output_weight, zero_first, scale_second, shift_second, swish_weight, linear_weight,
         down_weight, zero_second,
     )
-    small_all = lax.all_gather(pack_small(small, width), "samp", axis=0)
-    early_all = lax.all_gather(pack_rows(early, width), "samp", axis=0)
+    spans = lax.axis_size("head")
     late_all = lax.all_gather(pack_rows(late, width), "samp", axis=0)
-    (gain_one, bias_one, bias_query, bias_zero_one, gain_two, bias_two, bias_zero_two, pair_proj_w) = (
-        unpack_small(small_all, [piece.shape for piece in small])
-    )
-    (w_scale, w_shift, w_query, w_key, w_value, w_gate) = unpack_rows(
-        early_all, [piece.shape for piece in early]
-    )
+    mine = lax.broadcasted_iota(jnp.int32, (count, 1), 0) == lax.axis_index("samp")
+
+    def spread(piece, columns):
+        held = jnp.where(mine, piece[None], jnp.zeros_like(piece[None])).reshape(1, -1)
+        return jnp.pad(held, ((0, 0), (0, columns - held.shape[1])))
+
+    even_odd = jnp.concatenate((pair_weight[:, 0::2], pair_weight[:, 1::2]), axis=1).T
+    held = jnp.where(mine.reshape(1, count, 1), even_odd[:, None], jnp.zeros_like(even_odd[:, None]))
+    held = jnp.pad(held.reshape(even_odd.shape[0], -1), ((0, 0), (0, width - LANES)))
+    packed_small = jnp.concatenate(
+        [spread(piece, width) for piece in small] + [jnp.zeros((1, width), BF16), held], axis=0
+    )
+    (attended, prob, adapted, sig_first, gate_sig, query_split, key_value, full, *early_whole) = front(
+        struct_of, struct_len, act.reshape(total, width), cond.reshape(total, cond_width), packed_small,
+        pair, early, samples, count, spans,
+    )
+    (w_scale, w_shift, w_key, w_value, w_query, w_gate) = [
+        whole.reshape(-1, width) for whole in early_whole
+    ]
+    gain_one, bias_zero_one, gain_two = full[0, :cond_width], full[3], full[4, :cond_width]
+    bias_two, bias_zero_two = full[5], full[6]
+    heads = width // HEAD_DIM
+    pair_proj_w = full[8:, :LANES].reshape(2, heads // 2, -1).transpose(2, 1, 0).reshape(-1, heads).astype(BF16)
     (w_out, w_zero, w_scale_two, w_shift_two, w_swish, w_linear, w_down, w_zero_two) = unpack_rows(
         late_all, [piece.shape for piece in late]
     )
 
     pair_normed, pair_inverse = norm_rows(pair.astype(F32))
     pair_low = pair_normed.astype(BF16)
-    pair_proj = jnp.einsum("sijc,ch->shij", pair_low, pair_proj_w, preferred_element_type=F32)
-    packed = lax.all_gather(pack_bias(pair_proj.astype(BF16)), "samp", axis=0)
-
     act_rows = act.reshape(total, width).astype(F32)
     cond_low = cond.reshape(total, cond_width)
     act_normed, act_inverse = norm_rows(act_rows)
     cond_normed, cond_inverse = norm_rows(cond_low.astype(F32))
     cond_first = (cond_normed * gain_one.astype(F32)).astype(BF16)
-    sig_first = jax.nn.sigmoid(product(cond_first, w_scale) + bias_one.astype(F32))
-    adapted = (sig_first * act_normed + product(cond_first, w_shift)).astype(BF16)
-    key_rows = product(adapted, w_key).astype(BF16)
-    value_rows = product(adapted, w_value).astype(BF16)
-    query_rows = (product(adapted, w_query) + bias_query.astype(F32)).astype(BF16)
-    gate_sig = jax.nn.sigmoid(product(adapted, w_gate))
-    key_value = jnp.stack(
-        [key_rows_order(half.reshape(samples, rows, width), block) for half in (key_rows, value_rows)]
-    )
-    key_value = lax.all_gather(key_value, "head", axis=0)
-    query_split = query_rows.reshape(samples, rows, width)
-    attended, prob = attend(struct_of, struct_len, query_split, key_value, packed)
     attn_float = attended.reshape(total, width).astype(F32)
 
     gated_rows = (gate_sig * attn_float).astype(BF16)
@@ -1037,9 +1335,9 @@
     early_grads = (
         outer_sum(cond_first, d_pre_first),
         outer_sum(cond_first, d_shift_first),
-        outer_sum(adapted, d_query),
         outer_sum(adapted, d_key),
         outer_sum(adapted, d_value),
+        outer_sum(adapted, d_query),
         outer_sum(adapted, d_gate),
     )
     small_grads = (
@@ -1075,11 +1373,11 @@
     (g_out, g_zero, g_scale_two, g_shift_two, g_swish, g_linear, g_down, g_zero_two) = unpack_rows(
         late_sum[None], [piece.shape for piece in late]
     )
-    (g_scale, g_shift, g_query, g_key, g_value, g_gate) = unpack_rows(
+    (g_scale, g_shift, g_key, g_value, g_query, g_gate) = unpack_rows(
         early_sum[None], [piece.shape for piece in early]
     )
     (g_gain, g_bias, g_bias_query, g_bias_zero, g_gain_two, g_bias_two, g_bias_zero_two, g_pair) = (
-        unpack_small(small_sum, [piece.shape for piece in small])
+        unpack_small(small_sum, [piece.shape for piece in small + (pair_weight,)])
     )
     return (
         layer_out.reshape(act.shape), input_grad.reshape(act.shape), cond_grad.reshape(cond.shape),

time: 687 us -> 608 us (0.89)
  waiting for transfers between devices: 195 us -> 63.9 us
  Pallas kernels: 104 us -> 229 us
  local copies, waits for them, and re-layouts: 146 us -> 109 us
  matrix products: 105 us -> 87 us
  blocking collectives: 48.7 us -> 36.5 us
    pallas_call x1, Pallas kernels: 20.9 us -> 147 us  [front(): pl.pallas_call(front_kernel, out_shape=(jax.ShapeDtypeStruct((samples, ro...]
    all_gather x3 -> x0, waiting for transfers between devices: 89 us -> none  [the longest x1 68.9 us: per_device(): key_value = lax.all_gather(key_value, 'head', axis=0)]
    all_gather x1, waiting for transfers between devices: 40.8 us -> 0.01 us  [per_device(): late_all = lax.all_gather(pack_rows(late, width), 'samp', axis=0)]
    dot_general x1 -> x0, matrix products: 14.6 us -> none  [per_device(): jnp.einsum('sijc,ch->shij', pair_low, pair_proj_w, preferred_element_type...]
    reshape x5 -> x1, local copies, waits for them, and re-layouts: 12.2 us -> 1.24 us  [unpack_bias(): packed[pairs:, :, :MAIN].reshape(structs, rows, -1, heads)]
    all_gather x1 -> x0, blocking collectives: 10.9 us -> none  [per_device(): small_all = lax.all_gather(pack_small(small, width), 'samp', axis=0)]
    unnamed x246 -> x157, local copies, waits for them, and re-layouts: 59.9 us -> 50.7 us
    slice x6 -> x4, local copies, waits for them, and re-layouts: 13.9 us -> 10.6 us  [unpack_rows(): whole.append(gathered[:, at:at + held].reshape(count * rows, cols))]
  transfers between devices with their start and end apart: 7 -> 4, of which waited for: 4 -> 1; matrix products, arithmetic and copies ran while one was open for 33% -> 30% of each run, Pallas kernels for 3% -> 24%
where the time goes in v2:
time: 608 us; the launch traced here: 602 us
  Pallas kernels  229 us (38%)
  local copies, waits for them, and re-layouts  109 us (18%)
  matrix products  87 us (14%)
  waiting for transfers between devices  63.9 us (11%)
  other arithmetic  61.5 us (10%)
  blocking collectives  36.5 us (6%)
  between operations  15.1 us (2%)
    pallas_call x1, Pallas kernels, front(): pl.pallas_call(front_kernel, out_shape=(jax.ShapeDtypeStruct((samples, ro...  147 us
    pallas_call x1, Pallas kernels, attend_back(): pl.pallas_call(attend_back_kernel, out_shape=(jax.ShapeDtypeStruct((sampl...  82.2 us
    psum x1, waiting for transfers between devices, reduce(): return lax.psum(summed[0], 'head').astype(F32)  63.9 us
    unnamed x157, local copies, waits for them, and re-layouts  50.7 us
    dot_general x1, matrix products, per_device(): jnp.einsum('shij,ch->sijc', bias_summed, pair_proj_w, preferred_element_t...  30.3 us
    convert_element_type x1, other arithmetic, per_device(): pair_low = pair_normed.astype(BF16)  28.3 us
    unnamed x1, blocking collectives  22.4 us
    dot_general x1, matrix products, per_device(): jnp.einsum('sijc,shij->ch', pair_low, bias_summed, preferred_element_type...  18.5 us
  transfers between devices with their start and end apart: 4, of which 1 were waited for; matrix products, arithmetic and copies ran while one was open for 30% of the time, Pallas kernels for 24%

profile of v2, /device:TPU:0, one launch (start us, length us, event | category | flops | bytes accessed | tf_op | source)
XLA Modules:
  0.0 602.4 jit_solution(1875227349297675894)
XLA Ops:
  17.3 7.1 %copy.75.pair_ref = bf16[3,136,68,128]{3,2,1,0:T(8,128)(2,1)} copy(bf16[3,136,68,128]{3,1,2,0:T(8,128)(2,1)} %param.30) | data formatting | bytes 14204928 | tf_op args[2]
  25.8 146.6 %front.1 = (bf16[2,136,768]{2,1,0:T(8,128)(2,1)}, bf16[2,16,136,640]{3,2,1,0:T(8,128)(2,1)}, bf16[272,768]{1,0:T(8,128)(2,1)}, f32[272,768]{1,0:T(8,128)}, f32[2...) custom-call(s32[2]{0:T(128)} %struct_ref.3, ...), custom_call_target="tpu_custom_call" | custom-call | tf_op jit(solution)/shard_map/front/pallas_call | solution.py:545
  174.3 2.1 fusion.49
  177.7 2.8 fusion.85
  180.5 6.4 %fusion.84 = (bf16[8,192,768]{2,1,0:T(8,128)(2,1)}, bf16[8,192,768]{2,1,0:T(8,128)(2,1)}, bf16[8,192,768]{2,1,0:T(8,128)(2,1)}) fusion(bf16[8,864,768]{2,1,0:T(8,128)(2,1)} %bitcast.209), kind=kLoop, calls=%fused_computation.213 | loop fusion | bytes 14155776 | tf_op jit(solution)/shard_map/slice | solution.py:842
  186.9 4.8 reshape.639
  191.6 5.0 reshape.638
  217.2 82.2 %attend_back.1 = (bf16[2,136,768]{2,1,0:T(8,128)(2,1)}, bf16[2,2,136,768]{3,2,1,0:T(8,128)(2,1)}, bf16[27,136,128]{2,1,0:T(8,128)(2,1)}) custom-call(s32[2]{0:T(128)} %struct_ref.3, bf16[2,136,768]{2,1,0:T(8,128)(2,1)} %get-tuple-element.46.q_ref, bf16[4,2,2,136,768]{4,3,2,1,0:T(8,128)(2,1)} %get-tuple-element.47.kv_ref, bf16[2,136,768]{2,1,0:T(8,128)(2,1)} %bitcast.230, ...), custom_call_target="tpu_custom_call" | custom-call | tf_op jit(solution)/shard_map/attend_back/pallas_call | solution.py:791
  320.8 3.8 convolution_convert_fusion.1
  324.6 4.9 reshape.683
  329.6 4.1 convolution_convert_fusion.2
  333.7 4.9 reshape.682
  338.6 1.9 convolution_convert_fusion.3
  355.9 10.1 %convert_reduce_fusion = f32[3,136,68]{2,1,0:T(8,128)S(1)} fusion(bf16[3,136,68,128]{3,1,2,0:T(8,128)(2,1)} %param.30), kind=kLoop, calls=%fused_computation.1 | loop fusion | flops 7074720 | bytes 7213440 | tf_op jit(solution)/shard_map/reduce_sum | solution.py:22
  366.0 13.6 %fusion.8 = f32[3,136,68]{2,1,0:T(8,128)S(1)} fusion(f32[3,136,68]{2,1,0:T(8,128)S(1)} %broadcast_multiply_fusion.2, bf16[3,136,68,128]{3,1,2,0:T(8,128)(2,1)} %param.30), kind=kLoop, calls=%fused_computation.10 | loop fusion | flops 14177184 | bytes 7324416 | tf_op jit(solution)/shard_map/reduce_sum | solution.py:23
  382.8 3.4 reshape.654
  386.2 2.4 copy.77
  389.8 30.3 %fusion.71 = (f32[3,136,68]{2,1,0:T(8,128)S(1)}, f32[3,136,68]{2,1,0:T(8,128)S(1)}, f32[3,136,68,128]{3,2,1,0:T(8,128)S(1)}) fusion(f32[3,136,68]{2,1,0:T(8,128)} %add_rsqrt_fusion, f32[3,136,68]{2,1,0:T(8,128)S(1)} %broadcast_multiply_fusion.2, bf16[3,136,68,128]{3,1,2,0:T(8,128)(2,1)} %param.30, bf16[128,16,1,1]{0,1,3,2:T(8,128)(2,1)S(1)} %bitcast.258, ...), kind=kOutput, calls=%fused_computation.204 | convolution fusion | flops 136666944 | bytes 22643200 | tf_op jit(solution)/shard_map/shij,ch->sijc/dot_general | solution.py:1315
  420.3 28.3 %fusion.2 = (bf16[3,136,68,128]{3,2,1,0:T(8,128)(2,1)S(1)}, f32[3,136,68,128]{3,2,1,0:T(8,128)}) fusion(f32[3,136,68]{2,1,0:T(8,128)S(1)} %copy-done.39, f32[3,136,68]{2,1,0:T(8,128)S(1)} %broadcast_multiply_fusion.2, bf16[3,136,68,128]{3,1,2,0:T(8,128)(2,1)S(1)} %bitcast.196, f32[3,136,68]{2,1,0:T(8,128)S(1)} %broadcast_multiply_fusion, ...), kind=kLoop, calls=%fused_computation.4 | loop fusion | flops 28409856 | bytes 43058688 | tf_op jit(solution)/shard_map/convert_element_type | solution.py:1251
  448.6 18.5 %fusion.32 = bf16[128,16]{0,1:T(8,128)(2,1)S(1)} fusion(bf16[3,136,68,128]{3,2,1,0:T(8,128)(2,1)S(1)} %get-tuple-element.178, bf16[3,16,136,4]{3,1,2,0:T(8,128)(2,1)S(1)} %bitcast.238, bf16[3,16,136,64]{3,1,2,0:T(8,128)(2,1)S(1)} %bitcast.240), kind=kOutput, calls=%fused_computation.69 | convolution fusion | flops 115417088 | bytes 7994368 | tf_op jit(solution)/shard_map/sijc,shij->ch/dot_general | solution.py:1314
  467.4 22.4 %all-reduce.3 = bf16[8,832]{1,0:T(8,128)(2,1)S(1)} all-reduce(bf16[8,832]{1,0:T(8,128)(2,1)S(1)} %concatenate.33), channel_id=3, replica_groups=mesh['samp'=8,'head'=4] {'samp'}, use_global_device_ids=true, to_apply=%region_23.24.clone | all-reduce | flops 6656 | bytes 26624
  490.5 14.1 %psum.21 = bf16[1,832]{1,0:T(2,128)(2,1)S(1)} all-reduce(bf16[1,832]{1,0:T(2,128)(2,1)S(1)} %constant_dynamic-slice_fusion), channel_id=1, replica_groups=mesh['samp'=8,'head'=4] {'head'}, use_global_device_ids=true, to_apply=%region_24.25 | all-reduce | flops 832 | bytes 3328 | tf_op jit(solution)/shard_map/psum | solution.py:1370
  506.0 13.5 %copy.84 = f32[3,136,68,128]{3,1,2,0:T(8,128)} copy(f32[3,136,68,128]{3,2,1,0:T(8,128)} %get-tuple-element.179) | data formatting | bytes 28409856
  524.1 63.9 %all-reduce.7.cloned.1.call-done = (bf16[1,480,768]{2,1,0:T(8,128)(2,1)}, bf16[1,864,768]{2,1,0:T(8,128)(2,1)}) async-done(((bf16[1,480,768]{2,1,0:T(8,128)(2,1)}, bf16[1,864,768]{2,1,0:T(8,128)(2,1)}), (bf16[1,480,768]{2,1,0:T(8,128)(2,1)}, bf16[1,864,768]{2,1,0:T(8,128)(2,1)})) %all-reduce.7.cloned.1.call-update) | async-done | bytes 2064400 | tf_op jit(solution)/shard_map/psum | solution.py:1363
  (300 shorter events, 90.2 us)
Async XLA Ops:
  7.2 6.1 %copy-start.48 = (bf16[192,768]{1,0:T(8,128)(2,1)S(1)}, bf16[192,768]{1,0:T(8,128)(2,1)}, u32[]{:S(2)}) copy-start(bf16[192,768]{1,0:T(8,128)(2,1)} %param.52) | copy-start | bytes 884740
  7.2 6.2 %copy-start.49 = (bf16[48,768]{1,0:T(8,128)(2,1)S(1)}, bf16[48,768]{1,0:T(8,128)(2,1)}, u32[]{:S(2)}) copy-start(bf16[48,768]{1,0:T(8,128)(2,1)} %param.53) | copy-start | bytes 221188
  7.2 169.1 %all-gather.3.cloned.1.call-start = ((), (), s32[]{:S(2)}) async-start(), calls=%async_computation.4 | async-start | bytes 11943936 | tf_op jit(solution)/shard_map/all_gather | solution.py:1222
  8.4 6.2 %copy-start.50 = (bf16[16,16]{1,0:T(8,128)(2,1)S(1)}, bf16[16,16]{1,0:T(8,128)(2,1)}, u32[]{:S(2)}) copy-start(bf16[16,16]{1,0:T(8,128)(2,1)} %param.43) | copy-start | bytes 1540
  8.4 6.5 %copy-start.2 = (bf16[2,136,768]{2,1,0:T(8,128)(2,1)S(1)}, bf16[2,136,768]{2,1,0:T(8,128)(2,1)}, u32[]{:S(2)}) copy-start(bf16[2,136,768]{2,1,0:T(8,128)(2,1)} %param.28) | copy-start | bytes 1253380
  10.4 5.1 copy-start
  12.3 4.4 copy-start.53
  12.3 4.4 copy-start.54
  14.5 490.7 %reduce-scatter.3.cloned.1.call-start = ((), (), s32[]{:S(2)}) async-start(), calls=%async_computation.2 | async-start | bytes 6635520 | tf_op jit(solution)/shard_map/reduce_scatter | solution.py:1362
  25.8 148.3 %copy-start.1 = (bf16[2,136,384]{2,1,0:T(8,128)(2,1)S(1)}, bf16[2,136,384]{2,1,0:T(8,128)(2,1)}, u32[]{:S(2)}) copy-start(bf16[2,136,384]{2,1,0:T(8,128)(2,1)} %param.29) | copy-start | bytes 626692
  180.5 23.7 %copy-start.17 = (bf16[8,48,768]{2,1,0:T(8,128)(2,1)}, bf16[8,48,768]{2,1,0:T(8,128)(2,1)S(1)}, u32[]{:S(2)}) copy-start(bf16[8,48,768]{2,1,0:T(8,128)(2,1)S(1)} %get-tuple-element.176) | copy-start | bytes 1769476
  214.3 93.1 %copy-start.10 = (bf16[272,768]{1,0:T(8,128)(2,1)}, bf16[272,768]{1,0:T(8,128)(2,1)S(1)}, u32[]{:S(2)}) copy-start(bf16[272,768]{1,0:T(8,128)(2,1)S(1)} %get-tuple-element.160) | copy-start | bytes 1253380
  319.7 185.5 %reduce-scatter.5.cloned.1.call-start = ((), (), s32[]{:S(2)}) async-start(), calls=%async_computation.3 | async-start | bytes 11943936 | tf_op jit(solution)/shard_map/reduce_scatter | solution.py:1362
  324.6 4.9 copy-start.45
  333.7 4.9 copy-start.26
  354.5 233.5 %all-reduce.7.cloned.1.call-start = ((), (), s32[]{:S(2)}) async-start(), calls=%async_computation.5 | async-start | bytes 4128768 | tf_op jit(solution)/shard_map/psum | solution.py:1363
  366.0 14.3 %copy-start.29 = (bf16[2,136,768]{2,1,0:T(8,128)(2,1)S(1)}, bf16[2,136,768]{2,1,0:T(8,128)(2,1)}, u32[]{:S(2)}) copy-start(bf16[2,136,768]{2,1,0:T(8,128)(2,1)} %get-tuple-element.49) | copy-start | bytes 1253380
  366.0 14.4 %copy-start.38 = (bf16[27,136,128]{2,1,0:T(8,128)(2,1)S(1)}, bf16[27,136,128]{2,1,0:T(8,128)(2,1)}, u32[]{:S(2)}) copy-start(bf16[27,136,128]{2,1,0:T(8,128)(2,1)} %get-tuple-element.58) | copy-start | bytes 2820100
  382.8 5.7 copy-start.47
  389.8 30.4 %slice-start = ((s8[7102464]{0:T(1024)(128)(4,1)}), s8[4194304]{0:T(1024)(128)(4,1)S(1)}, s32[]{:S(2)}) async-start(s8[7102464]{0:T(1024)(128)(4,1)} %bitcast.195), calls=%async_computation.6 | async-start | bytes 8388608
  389.8 30.4 %slice-start.1 = ((s8[7102464]{0:T(1024)(128)(4,1)}), s8[2908160]{0:T(1024)(128)(4,1)S(1)}, s32[]{:S(2)}) async-start(s8[7102464]{0:T(1024)(128)(4,1)} %bitcast.195), calls=%async_computation.7 | async-start | bytes 5816320
  389.8 30.4 %copy-start.39 = (f32[3,136,68]{2,1,0:T(8,128)S(1)}, f32[3,136,68]{2,1,0:T(8,128)}, u32[]{:S(2)}) copy-start(f32[3,136,68]{2,1,0:T(8,128)} %add_rsqrt_fusion) | copy-start | bytes 332932
  420.3 28.3 %copy-start.31 = (bf16[3,8,2,136,64]{4,2,1,3,0:T(2,128)(2,1)S(1)}, bf16[3,8,2,136,64]{4,2,1,3,0:T(2,128)(2,1)}, u32[]{:S(2)}) copy-start(bf16[3,8,2,136,64]{4,2,1,3,0:T(2,128)(2,1)} %copy.77) | copy-start | bytes 2506756
  506.0 14.1 %copy-start.13 = (bf16[272,768]{1,0:T(8,128)(2,1)S(1)}, bf16[272,768]{1,0:T(8,128)(2,1)}, u32[]{:S(2)}) copy-start(bf16[272,768]{1,0:T(8,128)(2,1)} %get-tuple-element.198) | copy-start | bytes 1253380
  (47 other events, 94.2 us)
Sparse Core Ops, SparseCore 0:
  14.6 96.4 all-gather.2
  319.8 62.0 reduce-scatter.2
  386.0 82.2 reduce-scatter.4
  505.3 82.5 all-reduce.6

commit v3 on v2

--- a/solution.py
+++ b/solution.py
@@ -85,32 +85,6 @@
 
 def dot_tn(left, right):
     return lax.dot_general(left, right, (((0,), (0,)), ((), ())), preferred_element_type=F32)
-
-
-def key_rows_order(rows, block):
-    pieces = rows.shape[1] // block
-    main = [rows[:, at * block : at * block + MAIN] for at in range(pieces)]
-    tail = [rows[:, at * block + MAIN : (at + 1) * block] for at in range(pieces)]
-    return jnp.concatenate(main + tail, axis=1)
-
-
-def key_rows_back(rows, block):
-    pieces = rows.shape[1] // block
-    tail = block - MAIN
-    parts = []
-    for at in range(pieces):
-        parts.append(rows[:, at * MAIN : (at + 1) * MAIN])
-        parts.append(rows[:, pieces * MAIN + at * tail : pieces * MAIN + (at + 1) * tail])
-    return jnp.concatenate(parts, axis=1)
-
-
-def unpack_bias(packed, structs, heads):
-    rows = packed.shape[1]
-    pairs = structs * heads // 2
-    main = packed[:pairs].reshape(structs, heads // 2, rows, 2, MAIN)
-    main = main.transpose(0, 1, 3, 2, 4).reshape(structs, heads, rows, MAIN)
-    tail = packed[pairs:, :, :MAIN].reshape(structs, rows, -1, heads).transpose(0, 3, 1, 2)
-    return jnp.concatenate((main, tail), axis=3)
 
 
 def tail_switch(count, heads, tail):
@@ -584,8 +558,97 @@
     )(struct_of, struct_len, act, cond, small, pair, *shards)
 
 
+class Halving:
+    def __init__(self, me, order, source, zones, send_sem, recv_sem):
+        self.me, self.order, self.source, self.zones = me, order, source, zones
+        self.send_sem, self.recv_sem = send_sem, recv_sem
+
+    def copies(self, step):
+        kept = flips(self.me, self.order[step + 1 :])
+        found = []
+        for at, spot in enumerate(kept):
+            if step == 0:
+                leaving = self.source.at[flip(spot, self.order[0])]
+            else:
+                leaving = self.zones[step - 1].at[2 * at + 1]
+            found.append(
+                send(
+                    leaving, self.zones[step].at[at], self.send_sem.at[step, at],
+                    self.recv_sem.at[step, at], dict(samp=flip(self.me, self.order[step])),
+                )
+            )
+        return found
+
+    def start(self, step):
+        for copy in self.copies(step):
+            copy.start()
+
+    def finish(self, step):
+        kept = flips(self.me, self.order[step + 1 :])
+        zone = self.zones[step]
+        for at, copy in enumerate(self.copies(step)):
+            copy.wait_recv()
+
+            def add(turn, carry, at=at):
+                lines = pl.ds(pl.multiple_of(turn * 16, 16), 16)
+                mine = self.source[kept[at], lines] if step == 0 else self.zones[step - 1][2 * at, lines]
+                zone[at, lines] = (zone[at, lines].astype(F32) + mine.astype(F32)).astype(BF16)
+                return carry
+
+            lax.fori_loop(0, zone.shape[1] // 16, add, 0)
+
+    def settle(self):
+        for step in range(len(self.order)):
+            for copy in self.copies(step):
+                copy.wait_send()
+
+
+def zone_shapes(shapes, count):
+    zones = []
+    for rows, columns in shapes:
+        size = count // 2
+        while size:
+            zones.append(pltpu.VMEM((size, rows, columns), BF16))
+            size //= 2
+    return zones
+
+
+def spans_of(shapes, columns, spans):
+    lines = []
+    for at, (rows, wide) in enumerate(shapes):
+        for half in range(wide // columns):
+            lines += [(at, row, half * columns) for row in range(0, rows, 8)]
+    each = len(lines) // spans
+    moves = []
+    for piece in range(spans):
+        row = 0
+        for at, start, lane in lines[piece * each : (piece + 1) * each]:
+            last = moves[-1] if moves else None
+            if last and last[0] == piece and last[2] == at and last[4] == lane and last[3] + last[5] == start:
+                moves[-1] = last[:5] + (last[5] + 8,)
+            else:
+                moves.append((piece, row, at, start, lane, 8))
+            row += 8
+    return (each * 8, moves)
+
+
 def attend_back_kernel(
-    struct_ref, q_ref, kv_ref, do_ref, prob_ref, dq_ref, dkv_ref, dpb_ref,
+    late_shapes, struct_ref, q_ref, kv_ref, do_ref, prob_ref, *refs
+):
+    lates, refs = refs[: len(late_shapes)], refs[len(late_shapes) :]
+    (dq_ref, dkv_ref, dpb_ref, late_out, *refs) = refs
+    steps = 3
+    late_zones, refs = refs[: steps * len(late_shapes)], refs[steps * len(late_shapes) :]
+    (late_send, late_recv, *refs) = refs
+    attend_back_body(
+        late_shapes, struct_ref, q_ref, kv_ref, do_ref, prob_ref, lates, dq_ref, dkv_ref, dpb_ref, late_out,
+        late_zones, late_send, late_recv, *refs
+    )
+
+
+def attend_back_body(
+    late_shapes, struct_ref, q_ref, kv_ref, do_ref, prob_ref, lates, dq_ref, dkv_ref, dpb_ref, late_out,
+    late_zones, late_send, late_recv,
     key_ref, value_ref, dq_acc, dk_acc, dv_acc, first_ref, tail_ref, part_ref, span_ref, pack_ref,
     got_zero, got_one, got_two, span_send, span_recv, pack_send, pack_recv,
 ):
@@ -607,6 +670,14 @@
     greet(
         [dict(samp=flip(me, bit)) for bit in sorted(orders[0])] + [dict(head=other) for other in others]
     )
+    movers = [
+        Halving(
+            me, orders[at % 2], lates[at], late_zones[3 * at : 3 * at + 3], late_send.at[at], late_recv.at[at]
+        )
+        for at in range(len(lates))
+    ]
+    for mover in movers:
+        mover.start(0)
     switch = tail_switch(count, heads, tail)
     key_ref[keys:] = jnp.zeros_like(key_ref[keys:])
     value_ref[keys:] = jnp.zeros_like(value_ref[keys:])
@@ -696,7 +767,11 @@
                 span_copy(place, sample, away).start()
         return carry
 
-    lax.fori_loop(0, width // group, one_group, 0)
+    for place in range(width // group):
+        one_group(place, 0)
+        for mover in movers:
+            mover.finish(place)
+            mover.start(place + 1)
 
     mixed = []
     for sample in range(samples):
@@ -751,6 +826,14 @@
             if step + 1 < len(orders[0]):
                 for copy in flights[step + 1][half]:
                     copy.start()
+        if step == 0:
+            for mover in movers:
+                mover.finish(2)
+            _, moves = spans_of(late_shapes, width, spans)
+            for piece, row, at, start, lane, size in moves:
+                late_out[piece, row : row + size] = movers[at].zones[2][
+                    0, start : start + size, lane : lane + width
+                ]
 
     def out(tile, carry):
         dpb_ref[tile] = pack_ref[me, tile]
@@ -776,9 +859,11 @@
         for half in stage:
             for copy in half:
                 copy.wait_send()
-
-
-def attend_back(struct_of, structs, query, key_value, upstream, prob, count):
+    for mover in movers:
+        mover.settle()
+
+
+def attend_back(struct_of, structs, query, key_value, upstream, prob, lates, count):
     samples, rows, width = query.shape
     spans = key_value.shape[0]
     heads = width // HEAD_DIM
@@ -788,16 +873,23 @@
     steps = count.bit_length() - 1
     vmem = pl.BlockSpec(memory_space=pltpu.VMEM)
     smem = pl.BlockSpec(memory_space=pltpu.SMEM)
+    late_shapes = [late.shape[1:] for late in lates]
+    each, _ = spans_of(late_shapes, width, spans)
+    dma = pltpu.SemaphoreType.DMA
     return pl.pallas_call(
-        attend_back_kernel,
+        functools.partial(attend_back_kernel, late_shapes),
         out_shape=(
             jax.ShapeDtypeStruct((samples, rows, width), BF16),
             jax.ShapeDtypeStruct((2, samples, rows, width), BF16),
             jax.ShapeDtypeStruct((tiles, rows, LANES), BF16),
+            jax.ShapeDtypeStruct((spans, each, width), BF16),
         ),
-        in_specs=[smem, vmem, vmem, vmem, vmem],
-        out_specs=[vmem, vmem, vmem],
-        scratch_shapes=[
+        in_specs=[smem] + [vmem] * (4 + len(lates)),
+        out_specs=[vmem] * 4,
+        scratch_shapes=zone_shapes(late_shapes, count)
+        + [
+            dma((len(lates), steps, count // 2)),
+            dma((len(lates), steps, count // 2)),
             pltpu.VMEM((KEY_LANES, group), BF16),
             pltpu.VMEM((KEY_LANES, group), BF16),
             pltpu.VMEM((rows, group), F32),
@@ -820,7 +912,403 @@
             vmem_limit_bytes=60 << 20, collective_id=1, has_side_effects=True
         ),
         name="attend_back",
-    )(struct_of, query, key_value, upstream, prob)
+    )(struct_of, query, key_value, upstream, prob, *lates)
+
+
+def pair_switch(heads):
+    lanes = heads * MAIN
+    source = lax.broadcasted_iota(jnp.int32, (lanes, lanes), 0)
+    target = lax.broadcasted_iota(jnp.int32, (lanes, lanes), 1)
+    return jnp.where(source % heads * MAIN + source // heads == target, 1.0, 0.0).astype(BF16)
+
+
+def spread_heads(matrix, keys):
+    channels, heads = matrix.shape
+    one = lax.broadcasted_iota(jnp.int32, (heads, keys * heads), 0)
+    two = lax.broadcasted_iota(jnp.int32, (heads, keys * heads), 1)
+    repeat = dot_nn(matrix, jnp.where(two % heads == one, 1.0, 0.0).astype(BF16))
+    owner = lax.broadcasted_iota(jnp.int32, (1, keys * heads), 1) // heads
+    return [jnp.where(owner == key, repeat, 0.0).astype(BF16) for key in range(keys)]
+
+
+def mean_pair():
+    one = lax.broadcasted_iota(jnp.int32, (2 * LANES, 2 * LANES), 0) // LANES
+    two = lax.broadcasted_iota(jnp.int32, (2 * LANES, 2 * LANES), 1) // LANES
+    return jnp.where(one == two, 1.0 / LANES, 0.0).astype(BF16)
+
+
+def norm_pair(low, means):
+    centered = low.astype(F32) - dot_nn(low, means)
+    variance = dot_nn((centered * centered).astype(BF16), means)
+    inverse = lax.rsqrt(variance + EPSILON)
+    return (centered * inverse, inverse)
+
+
+GROUP = 16
+
+
+def finish_kernel(
+    early_shapes, late_shapes,
+    act_ref, cond_ref, adapted_ref, sig_ref, full_ref, dq_ref, dkv_ref, dgate_ref, dmid_ref, dcond_ref,
+    extra_ref, vector_ref, dpb_ref, late_ref, pair_ref, scale_w, shift_w, key_w, value_w, query_w, gate_w,
+    *refs
+):
+    (ig_ref, cg_ref, pg_ref, small_out, *refs) = refs
+    early_out, refs = refs[: len(early_shapes)], refs[len(early_shapes) :]
+    late_out, refs = refs[: len(late_shapes)], refs[len(late_shapes) :]
+    grads, refs = refs[: len(early_shapes)], refs[len(early_shapes) :]
+    zones, refs = refs[: 3 * len(early_shapes)], refs[3 * len(early_shapes) :]
+    (
+        early_ref, early_got, late_got, early_all, late_all, small_ref, small_got, sum_ref, sum_got,
+        pair_buf, lead_ref, lead_turned, spread_ref, block_ref, tail_block, weight_acc,
+        pair_sem, block_sem, grad_send, grad_recv, late_send, late_recv, early_send, early_recv,
+        small_send, small_recv, sum_send, sum_recv,
+    ) = refs
+    total, width = act_ref.shape
+    count = grads[0].shape[0]
+    spans = late_ref.shape[0]
+    structs, block, rows, _ = pair_buf.shape
+    samples = total // rows
+    heads = width // HEAD_DIM
+    tail = block - MAIN
+    pieces = rows // block
+    pairs = heads // 2
+    me = lax.axis_index("samp")
+    my_span = lax.axis_index("head")
+    orders = reduce_orders(count)
+    peers = flips(me, sorted(orders[0]))
+    others = [lax.rem(my_span + away, spans) for away in range(1, spans)]
+
+    loads = [
+        pltpu.make_async_copy(pair_ref.at[struct], pair_buf.at[struct], pair_sem.at[struct])
+        for struct in range(structs)
+    ]
+    for load in loads:
+        load.start()
+    greet([dict(samp=peer) for peer in peers[1:]] + [dict(head=other) for other in others])
+
+    def span_scatter(source, got, sems):
+        return [
+            send(source.at[other], got.at[at], sems[0].at[0, at], sems[1].at[0, at], dict(head=other))
+            for at, other in enumerate(others)
+        ]
+
+    def span_spread(whole, sems):
+        return [
+            send(whole.at[my_span], whole.at[my_span], sems[0].at[1, at], sems[1].at[1, at], dict(head=other))
+            for at, other in enumerate(others)
+        ]
+
+    def span_add(source, got, whole):
+        def add(turn, carry):
+            lines = pl.ds(pl.multiple_of(turn * 8, 8), 8)
+            summed = source[my_span, lines].astype(F32)
+            for at in range(spans - 1):
+                summed = summed + got[at, lines].astype(F32)
+            whole[my_span, lines] = summed.astype(BF16)
+            return carry
+
+        lax.fori_loop(0, source.shape[1] // 8, add, 0)
+
+    late_sems = (late_send, late_recv)
+    early_sems = (early_send, early_recv)
+    for copy in span_scatter(late_ref, late_got, late_sems):
+        copy.start()
+
+    adapted = adapted_ref[...]
+    back = one_hot((rows, rows), lambda row: row)
+    place = lax.broadcasted_iota(jnp.int32, (rows, rows), 1)
+    row = lax.broadcasted_iota(jnp.int32, (rows, rows), 0)
+    back = jnp.where(row == key_row_of(place, block, pieces), 1.0, 0.0).astype(BF16)
+    d_query = jnp.concatenate([dq_ref[at].astype(F32) for at in range(samples)], axis=0).astype(BF16)
+    d_key, d_value = [
+        jnp.concatenate([dot_nn(back, dkv_ref[which, at]) for at in range(samples)], axis=0).astype(BF16)
+        for which in range(2)
+    ]
+    d_gate = dgate_ref[...]
+
+    def store_grad(at, left, right):
+        size = grads[at].shape[1]
+        value = dot_tn(left, right).astype(BF16)
+        for owner in range(count):
+            grads[at][owner] = value[owner * size : (owner + 1) * size]
+
+    movers = [
+        Halving(
+            me, orders[at % 2], grads[at], zones[3 * at : 3 * at + 3], grad_send.at[at], grad_recv.at[at]
+        )
+        for at in range(len(grads))
+    ]
+    for at, upstream in ((2, d_key), (3, d_value), (4, d_query), (5, d_gate)):
+        store_grad(at, adapted, upstream)
+        movers[at].start(0)
+
+    d_adapted = dot_nt(d_query, query_w[...].reshape(-1, width))
+    d_adapted += dot_nt(d_key, key_w[...].reshape(-1, width))
+    d_adapted += dot_nt(d_value, value_w[...].reshape(-1, width))
+    d_adapted += dot_nt(d_gate, gate_w[...].reshape(-1, width))
+    gain_one = full_ref[0:1, : cond_ref.shape[1]]
+    act_normed, act_inverse = norm_rows(act_ref[...].astype(F32))
+    cond_normed, cond_inverse = norm_rows(cond_ref[...].astype(F32))
+    cond_first = (cond_normed * gain_one).astype(BF16)
+    sig_first = sig_ref[...]
+    d_shift = d_adapted.astype(BF16)
+    d_pre = (d_adapted * act_normed * sigmoid_slope(sig_first)).astype(BF16)
+    store_grad(0, cond_first, d_pre)
+    store_grad(1, cond_first, d_shift)
+    movers[0].start(0)
+    movers[1].start(0)
+    ig_ref[...] = dmid_ref[...] + norm_back(act_normed, act_inverse, d_adapted * sig_first)
+    d_cond = dot_nt(d_shift, shift_w[...].reshape(-1, width)) + dot_nt(d_pre, scale_w[...].reshape(-1, width))
+    cg_ref[...] = norm_back(cond_normed, cond_inverse, d_cond * gain_one + dcond_ref[...]) + extra_ref[...]
+    small_ref[...] = vector_ref[...]
+    small_ref[0:1, : cond_ref.shape[1]] = jnp.sum(d_cond * cond_normed, axis=0, keepdims=True)
+    small_ref[1:2] = jnp.sum(d_pre.astype(F32), axis=0, keepdims=True)
+    small_ref[2:3] = jnp.sum(d_query.astype(F32), axis=0, keepdims=True)
+
+    even_odd = full_ref[8:, :LANES]
+    one = lax.broadcasted_iota(jnp.int32, (heads, heads), 0)
+    two = lax.broadcasted_iota(jnp.int32, (heads, heads), 1)
+    natural = jnp.where(two == one // 2 + one % 2 * pairs, 1.0, 0.0).astype(BF16)
+    project = dot_nn(natural, even_odd.astype(BF16))
+    project = (project - jnp.mean(project, axis=1, keepdims=True)).astype(BF16)
+    eye = jnp.where(
+        lax.broadcasted_iota(jnp.int32, (LANES, LANES), 0) == lax.broadcasted_iota(jnp.int32, (LANES, LANES), 1),
+        1.0, 0.0,
+    ).astype(BF16)
+    columns = dot_nt(eye, project).astype(BF16)
+    for at, part in enumerate(spread_heads(columns, GROUP)):
+        spread_ref[at * LANES : (at + 1) * LANES] = part
+    switch = pair_switch(heads)
+    means = mean_pair()
+    groups = MAIN // GROUP
+    for struct in range(structs):
+        whole = jnp.concatenate([dpb_ref[struct * pairs + at] for at in range(pairs)], axis=1)
+        mixed = dot_nt(whole, switch).astype(BF16)
+        for at in range(groups):
+            lead_ref[struct * groups + at] = mixed[:, at * GROUP * heads : (at + 1) * GROUP * heads]
+    turn_eye = one_hot((rows, rows), lambda line: line)
+    weight_acc[...] = jnp.zeros_like(weight_acc)
+    for load in loads:
+        load.wait()
+
+    def back_keys(struct, first, keys, lead, target):
+        for at in range(keys // 2):
+            key = first + 2 * at
+            low = jnp.concatenate((pair_buf[struct, key], pair_buf[struct, key + 1]), axis=1)
+            normed, inverse = norm_pair(low, means)
+            upstream = dot_nt(lead, spread_ref[2 * at * LANES : (2 * at + 2) * LANES, : lead.shape[1]])
+            cross = dot_nn((upstream * normed).astype(BF16), means)
+            result = inverse * (upstream - normed * cross)
+            target(2 * at, result[:, :LANES])
+            target(2 * at + 1, result[:, LANES:])
+            kept = normed.astype(BF16)
+            for side in range(2):
+                turned = lead_turned[(2 * at + side) * heads : (2 * at + side + 1) * heads]
+                weight_acc[...] += dot_nn(turned, kept[:, side * LANES : (side + 1) * LANES])
+
+    def block_copy(turn):
+        slot = lax.rem(turn, 2)
+        return pltpu.make_async_copy(
+            block_ref.at[slot],
+            pg_ref.at[lax.div(turn, groups), pl.ds(lax.rem(turn, groups) * GROUP, GROUP)],
+            block_sem.at[slot],
+        )
+
+    def pair_group(turn, carry):
+        @pl.when(turn >= 2)
+        def _():
+            block_copy(turn - 2).wait()
+
+        slot = lax.rem(turn, 2)
+        lead = lead_ref[turn]
+        lead_turned[...] = dot_tn(lead, turn_eye).astype(BF16)
+
+        def target(at, value):
+            block_ref[slot, at] = value
+
+        back_keys(lax.div(turn, groups), lax.rem(turn, groups) * GROUP, GROUP, lead, target)
+        block_copy(turn).start()
+        return carry
+
+    turns = structs * groups
+    cuts = [turns * at // 6 for at in range(7)]
+    lax.fori_loop(cuts[0], cuts[1], pair_group, 0)
+    for at in range(len(movers)):
+        movers[at].finish(0)
+        movers[at].start(1)
+    for copy in span_scatter(late_ref, late_got, late_sems):
+        copy.wait_recv()
+    span_add(late_ref, late_got, late_all)
+    for copy in span_spread(late_all, late_sems):
+        copy.start()
+    lax.fori_loop(cuts[1], cuts[3], pair_group, 0)
+    for at in range(len(movers)):
+        movers[at].finish(1)
+        movers[at].start(2)
+    lax.fori_loop(cuts[3], cuts[5], pair_group, 0)
+    for at in range(len(movers)):
+        movers[at].finish(2)
+    _, moves = spans_of(early_shapes, width, spans)
+    for piece, line, at, start, lane, size in moves:
+        early_ref[piece, line : line + size] = movers[at].zones[2][0, start : start + size, lane : lane + width]
+    for copy in span_scatter(early_ref, early_got, early_sems):
+        copy.start()
+    lax.fori_loop(cuts[5], cuts[6], pair_group, 0)
+    for struct in range(structs):
+        lead = dpb_ref[structs * pairs + struct]
+        lead = lead[:, : tail * heads]
+        lead_turned[: tail * heads] = dot_tn(lead, turn_eye).astype(BF16)
+
+        def tail_target(at, value, struct=struct):
+            tail_block[struct, at] = value
+
+        back_keys(struct, MAIN, tail, lead, tail_target)
+    tail_copies = [
+        pltpu.make_async_copy(
+            tail_block.at[struct], pg_ref.at[struct, pl.ds(MAIN, tail)], pair_sem.at[struct]
+        )
+        for struct in range(structs)
+    ]
+    for copy in tail_copies:
+        copy.start()
+    small_ref[8:, :LANES] = weight_acc[...]
+
+    def small_copies(sending):
+        return [
+            send(
+                small_ref, small_got.at[me if sending else peers[at]], small_send.at[at], small_recv.at[at],
+                dict(samp=peers[at]),
+            )
+            for at in range(1, count)
+        ]
+
+    def sum_copies(sending):
+        return [
+            send(
+                sum_ref, sum_got.at[my_span if sending else lax.rem(my_span + spans - 1 - at, spans)],
+                sum_send.at[at], sum_recv.at[at], dict(head=other),
+            )
+            for at, other in enumerate(others)
+        ]
+
+    for copy in small_copies(True):
+        copy.start()
+    small_got[me] = small_ref[...]
+    for copy in small_copies(False):
+        copy.wait_recv()
+    summed = small_got[0]
+    for at in range(1, count):
+        summed = summed + small_got[at]
+    sum_ref[...] = summed
+    for copy in sum_copies(True):
+        copy.start()
+    sum_got[my_span] = summed
+    for copy in span_scatter(early_ref, early_got, early_sems):
+        copy.wait_recv()
+    span_add(early_ref, early_got, early_all)
+    for copy in span_spread(early_all, early_sems):
+        copy.start()
+    for copy in span_spread(late_all, late_sems):
+        copy.wait_recv()
+    _, late_moves = spans_of(late_shapes, width, spans)
+    for piece, line, at, start, lane, size in late_moves:
+        late_out[at][start : start + size, lane : lane + width] = late_all[piece, line : line + size].astype(F32)
+    for copy in sum_copies(False):
+        copy.wait_recv()
+    summed = sum_got[0]
+    for at in range(1, spans):
+        summed = summed + sum_got[at]
+    small_out[...] = summed
+    for copy in span_spread(early_all, early_sems):
+        copy.wait_recv()
+    for piece, line, at, start, lane, size in moves:
+        early_out[at][start : start + size, lane : lane + width] = early_all[piece, line : line + size].astype(F32)
+
+    block_copy(turns - 2).wait()
+    block_copy(turns - 1).wait()
+    for copy in tail_copies:
+        copy.wait()
+    for mover in movers:
+        mover.settle()
+    for copies in (
+        span_scatter(late_ref, late_got, late_sems), span_scatter(early_ref, early_got, early_sems),
+        span_spread(late_all, late_sems), span_spread(early_all, early_sems),
+        small_copies(True), sum_copies(True),
+    ):
+        for copy in copies:
+            copy.wait_send()
+
+
+def finish(
+    act, cond, adapted, sig, full, d_query, d_key_value, d_gate, d_middle, d_cond, extra, vectors, packed,
+    late, pair, weights, late_shapes,
+):
+    total, width = act.shape
+    cond_width = cond.shape[1]
+    spans, late_each, _ = late.shape
+    count = weights[0].shape[0]
+    structs, block, rows, _ = pair.shape
+    heads = width // HEAD_DIM
+    tail = block - MAIN
+    early_shapes = [weight.shape[1:] for weight in weights]
+    early_each, _ = spans_of(early_shapes, width, spans)
+    steps = count.bit_length() - 1
+    vmem = pl.BlockSpec(memory_space=pltpu.VMEM)
+    far = pl.BlockSpec(memory_space=pl.ANY)
+    dma = pltpu.SemaphoreType.DMA
+    turns = structs * (MAIN // GROUP)
+    return pl.pallas_call(
+        functools.partial(finish_kernel, early_shapes, late_shapes),
+        out_shape=(
+            jax.ShapeDtypeStruct((total, width), F32),
+            jax.ShapeDtypeStruct((total, cond_width), F32),
+            jax.ShapeDtypeStruct(pair.shape, F32),
+            jax.ShapeDtypeStruct(full.shape, F32),
+        )
+        + tuple(jax.ShapeDtypeStruct(shape, F32) for shape in list(early_shapes) + list(late_shapes)),
+        in_specs=[vmem] * 14 + [far] + [vmem] * 6,
+        out_specs=[vmem, vmem, far, vmem] + [vmem] * (len(early_shapes) + len(late_shapes)),
+        scratch_shapes=[pltpu.VMEM(weight.shape, BF16) for weight in weights]
+        + zone_shapes(early_shapes, count)
+        + [
+            pltpu.VMEM((spans, early_each, width), BF16),
+            pltpu.VMEM((spans - 1, early_each, width), BF16),
+            pltpu.VMEM((spans - 1, late_each, width), BF16),
+            pltpu.VMEM((spans, early_each, width), BF16),
+            pltpu.VMEM((spans, late_each, width), BF16),
+            pltpu.VMEM(full.shape, F32),
+            pltpu.VMEM((count,) + full.shape, F32),
+            pltpu.VMEM(full.shape, F32),
+            pltpu.VMEM((spans,) + full.shape, F32),
+            pltpu.VMEM(pair.shape, BF16),
+            pltpu.VMEM((turns, rows, GROUP * heads), BF16),
+            pltpu.VMEM((GROUP * heads, rows), BF16),
+            pltpu.VMEM((GROUP * LANES, GROUP * heads), BF16),
+            pltpu.VMEM((2, GROUP, rows, LANES), F32),
+            pltpu.VMEM((structs, tail, rows, LANES), F32),
+            pltpu.VMEM((heads, LANES), F32),
+            dma((structs,)),
+            dma((2,)),
+            dma((len(weights), steps, count // 2)),
+            dma((len(weights), steps, count // 2)),
+            dma((2, spans - 1)),
+            dma((2, spans - 1)),
+            dma((2, spans - 1)),
+            dma((2, spans - 1)),
+            dma((count,)),
+            dma((count,)),
+            dma((spans,)),
+            dma((spans,)),
+        ],
+        compiler_params=pltpu.CompilerParams(
+            vmem_limit_bytes=60 << 20, collective_id=3, has_side_effects=True
+        ),
+        name="finish",
+    )(
+        act, cond, adapted, sig, full, d_query, d_key_value, d_gate, d_middle, d_cond, extra, vectors, packed,
+        late, pair, *weights
+    )
 
 
 def pack_rows(pieces, columns):
@@ -1242,13 +1730,10 @@
     gain_one, bias_zero_one, gain_two = full[0, :cond_width], full[3], full[4, :cond_width]
     bias_two, bias_zero_two = full[5], full[6]
     heads = width // HEAD_DIM
-    pair_proj_w = full[8:, :LANES].reshape(2, heads // 2, -1).transpose(2, 1, 0).reshape(-1, heads).astype(BF16)
     (w_out, w_zero, w_scale_two, w_shift_two, w_swish, w_linear, w_down, w_zero_two) = unpack_rows(
         late_all, [piece.shape for piece in late]
     )
 
-    pair_normed, pair_inverse = norm_rows(pair.astype(F32))
-    pair_low = pair_normed.astype(BF16)
     act_rows = act.reshape(total, width).astype(F32)
     cond_low = cond.reshape(total, cond_width)
     act_normed, act_inverse = norm_rows(act_rows)
@@ -1293,6 +1778,10 @@
     d_gate = (d_gated * attn_float * sigmoid_slope(gate_sig)).astype(BF16)
     d_attended = (d_gated * gate_sig).astype(BF16)
 
+    def shares(grad, shape):
+        return grad.astype(BF16).reshape((count,) + shape)
+
+    order = (4, 5, 6, 0, 1, 2, 7, 3)
     late_grads = (
         outer_sum(gated_rows, d_branch),
         outer_sum(cond_low, d_zero_first),
@@ -1303,87 +1792,45 @@
         outer_sum(hidden, d_down),
         outer_sum(cond_low, d_zero_second),
     )
-
-    d_query, d_key_value, bias_packed = attend_back(
-        struct_of, structs, query_split, key_value, d_attended.reshape(samples, rows, width), prob, count
-    )
-    d_query = d_query.reshape(total, width)
-    d_key = key_rows_back(d_key_value[0], block).reshape(total, width)
-    d_value = key_rows_back(d_key_value[1], block).reshape(total, width)
-    bias_summed = unpack_bias(bias_packed, structs, width // HEAD_DIM)
-    pair_weight_grad = jnp.einsum("sijc,shij->ch", pair_low, bias_summed, preferred_element_type=F32)
-    pair_upstream = jnp.einsum(
-        "shij,ch->sijc", bias_summed, pair_proj_w, preferred_element_type=F32
-    )
-    pair_grad = norm_back(pair_normed, pair_inverse, pair_upstream)
-    d_adapted = (
-        back_product(d_query, w_query)
-        + back_product(d_key, w_key)
-        + back_product(d_value, w_value)
-        + back_product(d_gate, w_gate)
-    )
-    d_shift_first = d_adapted.astype(BF16)
-    d_pre_first = (d_adapted * act_normed * sigmoid_slope(sig_first)).astype(BF16)
-    d_cond_first = back_product(d_shift_first, w_shift) + back_product(d_pre_first, w_scale)
-    input_grad = d_middle + norm_back(act_normed, act_inverse, d_adapted * sig_first)
-    d_cond_normed = d_cond_first * gain_one.astype(F32) + d_cond_second * gain_two.astype(F32)
-    cond_grad = (
-        norm_back(cond_normed, cond_inverse, d_cond_normed)
-        + back_product(d_zero_first, w_zero)
-        + back_product(d_zero_second, w_zero_two)
-    )
-    early_grads = (
-        outer_sum(cond_first, d_pre_first),
-        outer_sum(cond_first, d_shift_first),
-        outer_sum(adapted, d_key),
-        outer_sum(adapted, d_value),
-        outer_sum(adapted, d_query),
-        outer_sum(adapted, d_gate),
-    )
-    small_grads = (
-        jnp.sum(d_cond_first * cond_normed, axis=0),
-        column_sum(d_pre_first),
-        column_sum(d_query),
-        column_sum(d_zero_first),
-        jnp.sum(d_cond_second * cond_normed, axis=0),
-        column_sum(d_pre_second),
-        column_sum(d_zero_second),
-        pair_weight_grad,
-    )
-
-    def pack_grads(grads, shapes):
-        pieces = [
-            grad.astype(BF16).reshape(count, shape[0] * shape[1] // width, width)
-            for grad, shape in zip(grads, shapes)
+    late_parts = [shares(late_grads[at], late[at].shape) for at in order]
+    d_query, d_key_value, bias_packed, late_sum = attend_back(
+        struct_of, structs, query_split, key_value, d_attended.reshape(samples, rows, width), prob,
+        late_parts, count,
+    )
+    d_cond_two = d_cond_second * gain_two
+    extra = back_product(d_zero_first, w_zero) + back_product(d_zero_second, w_zero_two)
+    vectors = jnp.stack(
+        [
+            column_sum(d_zero_first),
+            jnp.pad(jnp.sum(d_cond_second * cond_normed, axis=0), (0, width - cond_width)),
+            column_sum(d_pre_second),
+            column_sum(d_zero_second),
         ]
-        return jnp.concatenate(pieces, axis=1)
-
-    def reduce(packed):
-        summed = lax.psum_scatter(packed, "samp", scatter_dimension=0, tiled=True)
-        return lax.psum(summed[0], "head").astype(F32)
-
-    late_sum = reduce(pack_grads(late_grads, [piece.shape for piece in late]))
-    early_sum = reduce(pack_grads(early_grads, [piece.shape for piece in early]))
-    small_flat = jnp.concatenate(
-        [grad.astype(BF16).reshape(count, -1) for grad in small_grads], axis=1
-    )
-    small_sum = lax.psum(
-        lax.psum_scatter(small_flat, "samp", scatter_dimension=0, tiled=True), "head"
-    ).astype(F32)
-    (g_out, g_zero, g_scale_two, g_shift_two, g_swish, g_linear, g_down, g_zero_two) = unpack_rows(
-        late_sum[None], [piece.shape for piece in late]
-    )
-    (g_scale, g_shift, g_key, g_value, g_query, g_gate) = unpack_rows(
-        early_sum[None], [piece.shape for piece in early]
-    )
-    (g_gain, g_bias, g_bias_query, g_bias_zero, g_gain_two, g_bias_two, g_bias_zero_two, g_pair) = (
-        unpack_small(small_sum, [piece.shape for piece in small + (pair_weight,)])
-    )
+    )
+    vectors = jnp.pad(vectors, ((3, full.shape[0] - 7), (0, 0)))
+    (input_grad, cond_grad, pair_grad, small_sum, *weight_grads) = finish(
+        act.reshape(total, width), cond_low, adapted, sig_first, full, d_query, d_key_value, d_gate,
+        d_middle, d_cond_two, extra, vectors, bias_packed, late_sum, pair.transpose(0, 2, 1, 3),
+        early_whole, [late[at].shape for at in order],
+    )
+    (g_scale, g_shift, g_key, g_value, g_query, g_gate) = weight_grads[:6]
+    late_found = [None] * len(order)
+    for at, grad in zip(order, weight_grads[6:]):
+        late_found[at] = grad
+    (g_out, g_zero, g_scale_two, g_shift_two, g_swish, g_linear, g_down, g_zero_two) = late_found
+    mine_at = lax.axis_index("samp")
+
+    def own(row, size):
+        return lax.dynamic_slice(small_sum, (row, mine_at * size), (1, size))[0]
+
+    cond_share, share = cond_width // count, width // count
+    channels = pair.shape[3] // count
+    g_pair = lax.dynamic_slice(small_sum, (8, mine_at * channels), (heads, channels)).T
     return (
         layer_out.reshape(act.shape), input_grad.reshape(act.shape), cond_grad.reshape(cond.shape),
-        pair_grad, g_gain, g_scale, g_bias, g_shift, g_query, g_bias_query, g_key, g_value, g_gate,
-        g_out, g_pair, g_zero, g_bias_zero, g_gain_two, g_scale_two, g_bias_two, g_shift_two,
-        g_swish, g_linear, g_down, g_zero_two, g_bias_zero_two,
+        pair_grad.transpose(0, 2, 1, 3), own(0, cond_share), g_scale, own(1, share), g_shift, g_query,
+        own(2, share), g_key, g_value, g_gate, g_out, g_pair, g_zero, own(3, share), own(4, cond_share),
+        g_scale_two, own(5, share), g_shift_two, g_swish, g_linear, g_down, g_zero_two, own(6, share),
     )
 
 

time: 608 us -> 478 us (0.79)
  Pallas kernels: 229 us -> 352 us
  waiting for transfers between devices: 63.9 us -> 0.02 us
  other arithmetic: 61.5 us -> 4.67 us
  matrix products: 87 us -> 31.2 us
  local copies, waits for them, and re-layouts: 109 us -> 70.4 us
  blocking collectives: 36.5 us -> 0 us
    pallas_call x1 -> x2, Pallas kernels: 82.2 us -> 205 us  [the longest x1 106 us: finish(): pl.pallas_call(functools.partial(finish_kernel, early_shapes, late_shapes...]
    psum x1 -> x0, waiting for transfers between devices: 63.9 us -> none  [reduce(): return lax.psum(summed[0], 'head').astype(F32)]
    dot_general x2 -> x0, matrix products: 48.8 us -> none  [the longest x1 30.3 us: per_device(): jnp.einsum('shij,ch->sijc', bias_summed, pair_proj_w, preferred_element_t...]
    convert_element_type x2 -> x0, other arithmetic: 28.3 us -> none  [the longest x1 28.3 us: per_device(): pair_low = pair_normed.astype(BF16)]
    unnamed x1 -> x0, blocking collectives: 22.4 us -> none
    reshape x13 -> x0, local copies, waits for them, and re-layouts: 16.8 us -> none  [the longest x2 9.85 us: pack_grads(): grad.astype(BF16).reshape(count, shape[0] * shape[1] // width, width)]
    psum x1 -> x0, blocking collectives: 14.1 us -> none  [per_device(): lax.psum(lax.psum_scatter(small_flat, 'samp', scatter_dimension=0, tiled=...]
    reduce_sum x4 -> x2, other arithmetic: 14.4 us -> 0.52 us  [norm_rows(): variance = jnp.mean(centered * centered, axis=-1, keepdims=True)]
  transfers between devices with their start and end apart: 4 -> 1, of which waited for: 1 -> 0; matrix products, arithmetic and copies ran while one was open for 30% -> 3% of each run, Pallas kernels for 24% -> 31%
where the time goes in v3:
time: 478 us; the launch traced here: 473 us
  Pallas kernels  352 us (74%)
  local copies, waits for them, and re-layouts  70.4 us (15%)
  matrix products  31.2 us (7%)
  between operations  14.9 us (3%)
    pallas_call x1, Pallas kernels, front(): pl.pallas_call(front_kernel, out_shape=(jax.ShapeDtypeStruct((samples, ro...  147 us
    pallas_call x1, Pallas kernels, finish(): pl.pallas_call(functools.partial(finish_kernel, early_shapes, late_shapes...  106 us
    pallas_call x1, Pallas kernels, attend_back(): pl.pallas_call(functools.partial(attend_back_kernel, late_shapes), out_sh...  99.3 us
    unnamed x112, local copies, waits for them, and re-layouts  40.3 us
    dot_general x8, matrix products, outer_sum(): lax.dot_general(left_side, upstream, (((0,), (0,)), ((), ())), preferred_...  16.1 us
    slice x3, local copies, waits for them, and re-layouts, unpack_rows(): whole.append(gathered[:, at:at + held].reshape(count * rows, cols))  10.4 us
    reshape x2, local copies, waits for them, and re-layouts, unpack_rows(): whole.append(gathered[:, at:at + held].reshape(count * rows, cols))  9.71 us
  transfers between devices with their start and end apart: 1, of which 0 were waited for; matrix products, arithmetic and copies ran while one was open for 3% of the time, Pallas kernels for 31%

profile of v3, /device:TPU:0, one launch (start us, length us, event | category | flops | bytes accessed | tf_op | source)
XLA Modules:
  0.0 472.8 jit_solution(17897117986362490708)
XLA Ops:
  14.9 7.1 %copy.55.pair_ref = bf16[3,136,68,128]{3,2,1,0:T(8,128)(2,1)} copy(bf16[3,136,68,128]{3,1,2,0:T(8,128)(2,1)} %param.30) | data formatting | bytes 14204928 | tf_op args[2]
  23.3 146.6 %front.1 = (bf16[2,136,768]{2,1,0:T(8,128)(2,1)}, bf16[2,16,136,640]{3,2,1,0:T(8,128)(2,1)}, bf16[272,768]{1,0:T(8,128)(2,1)}, f32[272,768]{1,0:T(8,128)}, f32[2...) custom-call(s32[2]{0:T(128)} %struct_ref.3, ...), custom_call_target="tpu_custom_call" | custom-call | tf_op jit(solution)/shard_map/front/pallas_call | solution.py:519
  172.3 2.1 fusion.15
  174.4 1.3 slice.57
  175.8 2.6 fusion.40
  178.3 6.5 %fusion.39 = (bf16[8,192,768]{2,1,0:T(8,128)(2,1)}, bf16[8,192,768]{2,1,0:T(8,128)(2,1)}, bf16[8,192,768]{2,1,0:T(8,128)(2,1)}) fusion(bf16[8,864,768]{2,1,0:T(8,128)(2,1)} %bitcast.121), kind=kLoop, calls=%fused_computation.121 | loop fusion | bytes 14155776 | tf_op jit(solution)/shard_map/slice | solution.py:1330
  184.8 4.8 %reshape.424 = bf16[768,1536]{1,0:T(8,128)(2,1)} reshape(bf16[8,192,768]{2,1,0:T(8,128)(2,1)} %get-tuple-element.140) | data formatting | bytes 4718592 | tf_op jit(solution)/shard_map/reshape | solution.py:1330
  189.6 5.0 %reshape.423 = bf16[768,1536]{1,0:T(8,128)(2,1)} reshape(bf16[8,192,768]{2,1,0:T(8,128)(2,1)} %get-tuple-element.141) | data formatting | bytes 4718592 | tf_op jit(solution)/shard_map/reshape | solution.py:1330
  194.5 1.6 fusion.41
  203.7 1.4 multiply_convert_fusion
  207.2 1.9 convert_reduce_fusion
  210.6 1.5 fusion.17
  212.1 1.8 convolution_convert_fusion.3
  214.4 1.3 convolution_convert_fusion.7
  220.0 2.9 convolution_convert_fusion
  222.8 3.3 convolution_convert_fusion.1
  226.1 2.8 convolution_convert_fusion.2
  229.0 1.3 convolution_convert_fusion.5
  232.1 99.3 %attend_back.1 = (bf16[2,136,768]{2,1,0:T(8,128)(2,1)}, bf16[2,2,136,768]{3,2,1,0:T(8,128)(2,1)}, bf16[27,136,128]{2,1,0:T(8,128)(2,1)}, bf16[4,216,768]{2,1,0:T(8,128)(2,1)}) custom-call(s32[2]{0:T(128)} %struct_ref.3, bf16[2,136,768]{2,1,0:T(8,128)(2,1)} %get-tuple-element.67.q_ref, bf16[4,2,2,136,768]{4,3,2,1,0:T(8,128)(2,1)} %get-tuple-element.68.kv_ref, ...), custom_call_target="tpu_custom_call" | custom-call | tf_op jit(solution)/shard_map/attend_back/pallas_call | solution.py:879
  331.5 105.6 %finish.1 = (f32[272,768]{1,0:T(8,128)}, f32[272,384]{1,0:T(8,128)}, f32[3,68,136,128]{3,2,1,0:T(8,128)}, f32[24,768]{1,0:T(8,128)}, f32[48,768]{1,0:T(8,128)}, ...) custom-call(bf16[272,768]{1,0:T(8,128)(2,1)} %bitcast.143, ...), custom_call_target="tpu_custom_call" | custom-call | tf_op jit(solution)/shard_map/finish/pallas_call | solution.py:1261
  437.2 1.4 dynamic-slice_bitcast_fusion.3
  438.5 1.5 dynamic-slice_bitcast_fusion.1
  441.4 2.1 copy.81
  444.3 11.3 %copy.83 = f32[3,136,68,128]{3,1,2,0:T(8,128)} copy(f32[3,136,68,128]{3,1,2,0:T(8,128)} %bitcast.112) | data formatting | bytes 28409856
  (174 shorter events, 40.9 us)
Async XLA Ops:
  7.2 4.1 copy-start.32
  7.2 4.1 copy-start.33
  7.2 4.3 copy-start.20
  7.2 167.2 %all-gather.3.cloned.1.call-start = ((), (), s32[]{:S(2)}) async-start(), calls=%async_computation | async-start | bytes 11943936 | tf_op jit(solution)/shard_map/all_gather | solution.py:1710
  8.4 3.2 copy-start.34
  11.5 2.7 copy-start.38
  11.5 2.7 copy-start.39
  23.3 148.2 %copy-start.1 = (bf16[2,136,384]{2,1,0:T(8,128)(2,1)S(1)}, bf16[2,136,384]{2,1,0:T(8,128)(2,1)}, u32[]{:S(2)}) copy-start(bf16[2,136,384]{2,1,0:T(8,128)(2,1)} %param.29) | copy-start | bytes 626692
  178.3 17.7 %copy-start.7 = (bf16[8,48,768]{2,1,0:T(8,128)(2,1)}, bf16[8,48,768]{2,1,0:T(8,128)(2,1)S(1)}, u32[]{:S(2)}) copy-start(bf16[8,48,768]{2,1,0:T(8,128)(2,1)S(1)} %get-tuple-element.145) | copy-start | bytes 1769476
  209.1 3.1 copy-start.4
  437.1 6.4 %copy-start.19 = (f32[272,384]{1,0:T(8,128)S(1)}, f32[272,384]{1,0:T(8,128)}, u32[]{:S(2)}) copy-start(f32[272,384]{1,0:T(8,128)} %get-tuple-element.81) | copy-start | bytes 1253380
  444.3 11.4 %copy-start.31 = (f32[48,768]{1,0:T(8,128)S(1)}, f32[48,768]{1,0:T(8,128)}, u32[]{:S(2)}) copy-start(f32[48,768]{1,0:T(8,128)} %get-tuple-element.218) | copy-start | bytes 442372
  444.3 12.0 %copy-start.30 = (f32[48,768]{1,0:T(8,128)S(1)}, f32[48,768]{1,0:T(8,128)}, u32[]{:S(2)}) copy-start(f32[48,768]{1,0:T(8,128)} %get-tuple-element.220) | copy-start | bytes 442372
  444.3 12.7 %copy-start.25 = (f32[96,768]{1,0:T(8,128)S(1)}, f32[96,768]{1,0:T(8,128)}, u32[]{:S(2)}) copy-start(f32[96,768]{1,0:T(8,128)} %get-tuple-element.221) | copy-start | bytes 884740
  444.3 13.4 %copy-start.24 = (f32[96,768]{1,0:T(8,128)S(1)}, f32[96,768]{1,0:T(8,128)}, u32[]{:S(2)}) copy-start(f32[96,768]{1,0:T(8,128)} %get-tuple-element.223) | copy-start | bytes 884740
  455.7 2.8 copy-start.23
  455.7 3.5 copy-start.22
  455.7 4.2 copy-start.21
  456.3 4.3 copy-start.29
  457.0 4.3 copy-start.28
  457.0 4.9 %copy-start.27 = (f32[48,768]{1,0:T(8,128)S(1)}, f32[48,768]{1,0:T(8,128)}, u32[]{:S(2)}) copy-start(f32[48,768]{1,0:T(8,128)} %get-tuple-element.233) | copy-start | bytes 442372
  457.7 4.9 %copy-start.17 = (f32[96,1536]{1,0:T(8,128)S(1)}, f32[96,1536]{1,0:T(8,128)}, u32[]{:S(2)}) copy-start(f32[96,1536]{1,0:T(8,128)} %get-tuple-element.234) | copy-start | bytes 1769476
  459.2 4.2 copy-start.16
  460.6 3.6 copy-start.15
  (20 other events, 35.8 us)
Sparse Core Ops, SparseCore 0:
  12.8 95.6 all-gather.2
